TPU v7x, 512 devices: a whole 4x4x16 slice. The times are simulated.
512 devices in a mesh: teacher: 16 (over z_hi, x, core), vocab: 32 (over z_lo, y).
Axes of the slice: x: 4, y: 4, z: 16 (z_hi: 2, z_lo: 8; z = z_hi * 8 + z_lo), core: 2. Of those that a mesh axis runs over, the one named last changes fastest.
Arguments:
- teacher_hidden: bfloat16 [16, 128, 2048], P('teacher', 'vocab'), may hold values from -32 to 32
- teacher_head: bfloat16 [2048, 65536], P('teacher', 'vocab'), may hold values from -1 to 1
- student_hidden: bfloat16 [128, 2048], P(None, 'teacher'), may hold values from -32 to 32
- student_head: bfloat16 [2048, 65536], P('teacher', 'vocab'), may hold values from -1 to 1
- labels: int32 [128], P('teacher'), may hold values from 0 to 65535
Outputs:
- ce_matrix: float32 [128, 16, 16], P('teacher')
- agreement: float32 [128, 16], P('teacher')
- student_grad: float32 [2048, 65536], P('teacher', 'vocab')
All inputs are finite; a program needn't handle non-finite values.
Results may differ from a plain program's by a relative error of at most 0.0065.
Values may be sent and summed in bfloat16 or wider, within the bound.
A program may use at most 64 MiB of HBM per device.

v0:
```python
import jax
import jax.numpy as jnp
from jax import lax
from jax.sharding import PartitionSpec as P

HARD_SHARE = 0.3


def teacher_normalizer(logits):
    highest = lax.pmax(jnp.max(logits, axis=1), "vocab")
    summed = lax.psum(jnp.sum(jnp.exp(logits - highest[:, None]), axis=1), "vocab")
    return highest + jnp.log(summed)


def student_normalizer(logits):
    highest = lax.pmax(jnp.max(logits, axis=1), "vocab")
    summed = lax.psum(jnp.sum(jnp.exp(logits - highest[:, None]), axis=1), "vocab")
    return highest + jnp.log(summed)


def student_scores(student_hidden, student_head):
    return lax.psum_scatter(
        jnp.dot(student_hidden, student_head, preferred_element_type=jnp.float32),
        "teacher",
        scatter_dimension=0,
        tiled=True,
    )


def on_device(teacher_hidden, teacher_head, student_hidden, student_head, labels):
    teachers = lax.axis_size("teacher")
    block_rows = student_hidden.shape[0] // teachers
    shard_width = teacher_head.shape[1]
    gathered = lax.all_gather(teacher_hidden, "vocab", axis=1, tiled=True)
    flat_rows = gathered[0]
    columns = flat_rows
    logits = jnp.dot(
        columns,
        lax.all_gather(teacher_head, "teacher", axis=0, tiled=True),
        preferred_element_type=jnp.float32,
    )
    log_norm = teacher_normalizer(logits)
    log_prob = (logits - log_norm[:, None]).astype(jnp.bfloat16)
    exchanged = lax.all_to_all(log_prob[None], "teacher", split_axis=1, concat_axis=0, tiled=True)
    teacher_prob = jnp.exp(exchanged.astype(jnp.float32)).astype(jnp.bfloat16)
    cross_local = -jnp.einsum(
        "itv,jtv->tij", teacher_prob, exchanged, preferred_element_type=jnp.float32
    )
    cross_matrix = lax.psum(cross_local, "vocab")
    disagree = jnp.mean(cross_matrix, axis=1)
    inverse = 1.0 / (1.0 + disagree)
    weights = inverse / jnp.sum(inverse, axis=1, keepdims=True)
    soft_mix = jnp.sum(weights.T[:, :, None] * teacher_prob.astype(jnp.float32), axis=0)
    col_offset = lax.axis_index("vocab") * shard_width
    columns = lax.broadcasted_iota(jnp.int32, (block_rows, shard_width), 1) + col_offset
    onehot = (columns == labels[:, None]).astype(jnp.float32)
    target = (1.0 - HARD_SHARE) * soft_mix + HARD_SHARE * onehot
    student_logits = student_scores(student_hidden, student_head)
    student_norm = student_normalizer(student_logits)
    student_prob = jnp.exp(student_logits - student_norm[:, None])
    residual = (student_prob - target).astype(jnp.bfloat16)
    student_grad = lax.dot_general(
        student_hidden,
        lax.all_gather(residual, "teacher", axis=0, tiled=True),
        (((0,), (0,)), ((), ())),
        preferred_element_type=jnp.float32,
    )
    return (cross_matrix, weights * teachers, student_grad)


def solution(mesh):
    return jax.shard_map(
        on_device,
        mesh=mesh,
        in_specs=(
            P("teacher", "vocab", None),
            P("teacher", "vocab"),
            P(None, "teacher"),
            P("teacher", "vocab"),
            P("teacher"),
        ),
        out_specs=(P("teacher", None, None), P("teacher", None), P("teacher", "vocab")),
        check_vma=False,
    )
```

profile of v0, /device:TPU:1, one launch (start us, length us, event | category | flops | bytes accessed | tf_op | source)
XLA Modules:
  0.0 843.5 jit_solution(16325819775423183656)
XLA Ops:
  7.2 0.0 copy-start
  7.2 0.0 reduce-scatter.2.cloned.1.call-start
  7.2 1.0 copy-done
  8.2 2.0 fusion.7
  10.2 0.0 reduce-scatter.2.cloned.1.call-update
  10.2 0.0 all-gather.2.cloned.1.call-start
  10.3 0.7 all-gather.2.cloned.1.call-update
  11.0 0.7 copy.14
  11.8 122.6 %all_gather.9 = bf16[1,128,2048]{2,0,1:T(2,128)(2,1)S(1)} all-gather(bf16[1,4,2048]{2,0,1:T(2,128)(2,1)S(1)} %copy.14), channel_id=1, replica_groups=mesh['teacher'=16,'vocab'=32] {'vocab'}, dimensions={1}, use_global_device_ids=true | all-gather | bytes 540672 | tf_op jit(solution)/shard_map/all_gather | solution.py:34
  134.3 0.0 reduce-scatter.2.cloned.1.call-done
  134.3 1.0 reduce_max.19
  135.3 0.0 copy-start.1
  135.3 167.3 %all-gather.2.cloned.1.call-done = bf16[2048,2048]{1,0:T(8,128)(2,1)} async-done(((bf16[128,2048]{1,0:T(8,128)(2,1)}), bf16[2048,2048]{1,0:T(8,128)(2,1)}) %all-gather.2.cloned.1.call-update) | async-done | bytes 8388624 | tf_op jit(solution)/shard_map/all_gather | solution.py:39
  302.6 4.9 fusion.6
  307.5 0.0 copy-start.4
  307.6 0.0 copy-start.2
  307.6 100.2 %all-reduce.1 = (f32[128]{0:T(128)S(1)}, f32[8]{0:T(128)S(1)}) all-reduce(f32[128]{0:T(128)S(1)} %get-tuple-element.18, f32[8]{0:T(128)S(1)} %reduce_max.19), channel_id=1, replica_groups=mesh['teacher'=16,'vocab'=32] {'vocab'}, use_global_device_ids=true, to_apply=%region_1.0 | all-reduce | flops 136 | bytes 1088 | tf_op jit(solution)/shard_map/pmax | solution.py:10
  407.8 0.3 exponential_reduce_fusion
  408.1 103.4 %psum.21 = f32[128]{0:T(128)S(1)} all-reduce(f32[128]{0:T(128)S(1)} %exponential_reduce_fusion), channel_id=1, replica_groups=mesh['teacher'=16,'vocab'=32] {'vocab'}, use_global_device_ids=true, to_apply=%region_3.0 | all-reduce | flops 128 | bytes 1024 | tf_op jit(solution)/shard_map/psum | solution.py:11
  511.5 0.1 fusion
  511.6 0.8 copy.35
  512.5 0.5 broadcast.52
  513.0 3.7 reduce
  516.7 1.3 reshape.19
  518.0 34.5 %all-to-all-start = ((bf16[16,2,8192]{2,1,0:T(2,128)(2,1)}), bf16[16,2,8192]{2,1,0:T(2,128)(2,1)S(1)}, u32[]{:S(2)}, u32[]{:S(2)}) async-start(bf16[16,2,8192]{2,1,0:T(2,128)(2,1)} %reshape.19), calls=%async_computation | async-start | bytes 1048576 | tf_op jit(solution)/shard_map/all_to_all | solution.py:44
  552.6 0.0 copy-done.1
  552.6 0.2 exponential_reduce_fusion.1
  552.8 18.3 %all-to-all-done = bf16[16,2,8192]{2,1,0:T(2,128)(2,1)S(1)} async-done(((bf16[16,2,8192]{2,1,0:T(2,128)(2,1)}), bf16[16,2,8192]{2,1,0:T(2,128)(2,1)S(1)}, u32[]{:S(2)}, u32[]{:S(2)}) %all-to-all-start) | async-done | bytes 524320 | tf_op jit(solution)/shard_map/all_to_all | solution.py:44
  571.1 0.5 reshape.20
  571.6 0.3 copy.34
  571.9 0.5 convolution_negate_fusion
  572.4 196.4 %all-reduce = (f32[8,16,16]{2,1,0:T(8,128)S(1)}, f32[8]{0:T(128)S(1)}) all-reduce(f32[8,16,16]{2,1,0:T(8,128)S(1)} %convolution_negate_fusion, f32[8]{0:T(128)S(1)} %exponential_reduce_fusion.1), channel_id=1, replica_groups=mesh['teacher'=16,'vocab'=32] {'vocab'}, use_global_device_ids=true, to_apply=%region_4.0 | all-reduce | flops 2056 | bytes 16448 | tf_op jit(solution)/shard_map/psum | solution.py:49
  768.8 0.0 copy-start.3
  768.8 0.1 divide_reduce_fusion
  768.9 0.7 fusion.5
  769.6 0.5 multiply_reduce_fusion
  770.1 0.0 copy-done.4
  770.1 0.1 subtract_convert_fusion.1
  770.2 64.8 %all_gather.11 = bf16[128,2048]{1,0:T(8,128)(2,1)S(1)} all-gather(bf16[8,2048]{1,0:T(8,128)(2,1)S(1)} %subtract_convert_fusion.1), channel_id=1, replica_groups=mesh['teacher'=16,'vocab'=32] {'teacher'}, dimensions={0}, use_global_device_ids=true | all-gather | bytes 557056 | tf_op jit(solution)/shard_map/all_gather | solution.py:64
  835.0 0.0 copy-done.2
  835.0 0.3 convolution_bitcast_fusion
  835.3 1.3 copy.18
  836.7 0.0 copy-done.3
  (4 shorter events, 0.0 us)
Async XLA Ops:
  7.2 1.0 copy-start
  7.2 127.1 %reduce-scatter.2.cloned.1.call-start = ((), (), s32[]{:S(2)}) async-start(), calls=%async_computation.3 | async-start | bytes 1114112 | tf_op jit(solution)/shard_map/reduce_scatter | solution.py:22
  10.2 292.4 %all-gather.2.cloned.1.call-start = ((), (), s32[]{:S(2)}) async-start(), calls=%async_computation.2 | async-start | bytes 8912896 | tf_op jit(solution)/shard_map/all_gather | solution.py:39
  135.3 417.3 %copy-start.1 = (f32[8,2048]{1,0:T(8,128)S(1)}, f32[8,2048]{1,0:T(8,128)}, u32[]{:S(2)}) copy-start(f32[8,2048]{1,0:T(8,128)} %reduce-scatter.2.cloned.1.call-done) | copy-start | bytes 196612
  307.5 462.6 %copy-start.4 = (s32[8]{0:T(128)S(1)}, s32[8]{0:T(128)}, u32[]{:S(2)}) copy-start(s32[8]{0:T(128)} %param.9) | copy-start | bytes 100
  307.6 527.4 %copy-start.2 = (bf16[128,128]{1,0:T(8,128)(2,1)S(1)}, bf16[128,128]{1,0:T(8,128)(2,1)}, u32[]{:S(2)}) copy-start(bf16[128,128]{1,0:T(8,128)(2,1)} %param.7) | copy-start | bytes 98308
  518.0 53.0 %all-to-all-start = ((bf16[16,2,8192]{2,1,0:T(2,128)(2,1)}), bf16[16,2,8192]{2,1,0:T(2,128)(2,1)S(1)}, u32[]{:S(2)}, u32[]{:S(2)}) async-start(bf16[16,2,8192]{2,1,0:T(2,128)(2,1)} %reshape.19), calls=%async_computation | async-start | bytes 1048576 | tf_op jit(solution)/shard_map/all_to_all | solution.py:44
  768.8 67.9 %copy-start.3 = (f32[8,16,16]{2,1,0:T(8,128)}, f32[8,16,16]{2,1,0:T(8,128)S(1)}, u32[]{:S(2)}) copy-start(f32[8,16,16]{2,1,0:T(8,128)S(1)} %get-tuple-element.12) | copy-start | bytes 24580
Sparse Core Ops, SparseCore 0:
  13.3 111.9 reduce-scatter.1
  129.2 173.4 all-gather.1
where the time goes:
time: 844 us; the launch traced here: 843 us
  blocking collectives  587 us (70%)
  waiting for transfers between devices  186 us (22%)
  starting transfers between devices  34.6 us (4%)
  between operations  14.2 us (2%)
    psum x1, blocking collectives, on_device(): cross_matrix = lax.psum(cross_local, 'vocab')  196 us
    all_gather x1, waiting for transfers between devices, on_device(): lax.all_gather(teacher_head, 'teacher', axis=0, tiled=True)  167 us
    all_gather x1, blocking collectives, on_device(): gathered = lax.all_gather(teacher_hidden, 'vocab', axis=1, tiled=True)  123 us
    psum x1, blocking collectives, teacher_normalizer(): lax.psum(jnp.sum(jnp.exp(logits - highest[:, None]), axis=1), 'vocab')  103 us
    pmax x1, blocking collectives, teacher_normalizer(): highest = lax.pmax(jnp.max(logits, axis=1), 'vocab')  100 us
    all_gather x1, blocking collectives, on_device(): lax.all_gather(residual, 'teacher', axis=0, tiled=True)  64.8 us
    all_to_all x1, starting transfers between devices, on_device(): lax.all_to_all(log_prob[None], 'teacher', split_axis=1, concat_axis=0, ti...  34.5 us
    all_to_all x1, waiting for transfers between devices, on_device(): lax.all_to_all(log_prob[None], 'teacher', split_axis=1, concat_axis=0, ti...  18.3 us
  transfers between devices with their start and end apart: 3, of which 2 were waited for; matrix products, arithmetic and copies ran while one was open for 0% of the time, Pallas kernels for 0%

commit v1 on v0

v1 whole, which is shorter than its diff:
```python
import jax
import jax.numpy as jnp
from jax import lax
from jax.experimental import pallas as pl
from jax.experimental.pallas import tpu as pltpu
from jax.sharding import PartitionSpec as P

HARD_SHARE = 0.3
MESH = pl.DeviceIdType.MESH
F32 = jnp.float32
BF16 = jnp.bfloat16
I32 = jnp.int32


def iota(shape, dim):
    return lax.broadcasted_iota(I32, shape, dim)


def row_token(r):
    return (r >> 3) & 15


def row_teacher(r):
    return (r >> 7) * 8 + (r & 7)


def fold_tokens(values):
    same = row_token(iota((256, 256), 0)) == row_token(iota((256, 256), 1))
    kept = jnp.where(same, values, 0.0).reshape(2, 16, 8, 256)
    return jnp.sum(kept, axis=1).reshape(16, 256)


def own_lane(values):
    same = iota((16, 256), 0) == row_teacher(iota((16, 256), 1))
    return jnp.sum(jnp.where(same, values, 0.0), axis=0, keepdims=True)


def kernel(
    hid_in, head, sh, shead, lab_in,
    grad_out, ce_out, agree_out,
    W, relay, hx, hid, L, Eb, Cb, mbuf, sbuf,
    S, Sc, A, Sx, T, Sz, SL, lab, yb, xb, rb, gb, R,
    s_z, s_rf, s_xl, s_xf, s_c, s_h1, s_h2, s_h3, s_st, s_y, s_z1, s_z2, s_r,
    r_relay, r_w, r_h1, r_h2, r_sc, r_sx, r_sz, r_lab, r_y, r_z1, r_z2, r_r, l_w,
):
    t = lax.axis_index("teacher")
    v = lax.axis_index("vocab")
    zh, xc = t // 8, t % 8
    x, c = xc // 2, xc % 2
    zl, y = v // 4, v % 4
    z = zh * 8 + zl

    def dev(z_, xc_, y_):
        return {"teacher": (z_ // 8) * 8 + xc_, "vocab": (z_ % 8) * 4 + y_}

    def send(src, dst, ssem, rsem, to):
        pltpu.make_async_remote_copy(
            src_ref=src, dst_ref=dst, send_sem=ssem, recv_sem=rsem, device_id=to, device_id_type=MESH
        ).start()

    def done(ref, sem):
        pltpu.make_async_copy(ref, ref, sem).wait()

    def each(lo, hi, body):
        def step(i, carry):
            body(i)
            return carry
        lax.fori_loop(lo, hi, step, 0)

    z_to = lambda d: dev((z + d) % 16, xc, y)
    x_to = lambda d: dev(z, ((x + d) % 4) * 2 + c, y)
    y_to = lambda d: dev(z, xc, (y + d) % 4)
    xc_to = lambda d: dev(z, (xc + d) % 8, y)
    sibling = dev(z, x * 2 + 1 - c, y)
    partner = z_to(8)

    barrier = pltpu.get_barrier_semaphore()
    each(1, 16, lambda d: pl.semaphore_signal(barrier, inc=1, device_id=z_to(d), device_id_type=MESH))
    each(1, 8, lambda d: pl.semaphore_signal(barrier, inc=1, device_id=xc_to(d), device_id_type=MESH))
    each(1, 4, lambda d: pl.semaphore_signal(barrier, inc=1, device_id=y_to(d), device_id_type=MESH))
    pl.semaphore_wait(barrier, 25)

    mine = pl.ds(pl.multiple_of(zh * 1024, 1024), 1024)
    other = pl.ds(pl.multiple_of((1 - zh) * 1024, 1024), 1024)
    piece = lambda zh_, x_, c_, half: ((zh_ * 8 + x_ * 2 + c_) * 2) + half
    w_at = lambda p: W.at[pl.ds(pl.multiple_of(p * 64, 64), 64), :]

    for half, d in ((0, 4), (1, 12)):
        send(head.at[pl.ds(half * 64, 64), other], relay.at[half], s_z.at[half], r_relay.at[half], z_to(d))
    spread = (z % 4) * 2 + y // 2
    is_spread = xc == spread
    to_spread = dev(z, spread, y)

    @pl.when(is_spread)
    def _():
        pltpu.make_async_copy(hid_in, hx.at[xc], r_h1.at[xc]).start()

    @pl.when(jnp.logical_not(is_spread))
    def _():
        send(hid_in, hx.at[xc], s_h1.at[0], r_h1.at[xc], to_spread)

    for half in range(2):
        p = piece(zh, x, c, half)
        src = head.at[pl.ds(half * 64, 64), mine]
        send(src, w_at(p), s_xl.at[half * 2], r_w.at[p], x_to(1))
        send(src, w_at(p), s_xl.at[half * 2 + 1], r_w.at[p], x_to(3))
        send(src, w_at(p), s_c.at[p], r_w.at[p], sibling)
        pltpu.make_async_copy(src, w_at(p), l_w.at[half]).start()
    lab[pl.ds(zh, 1)] = lab_in[...][None]
    send(lab.at[zh], lab.at[zh], s_st.at[5], r_lab.at[0], partner)

    for k in range(4):
        cols = pl.ds(k * 512, 512)
        S[:, :, :, :, cols] = jnp.dot(sh[...], shead[:, cols], preferred_element_type=F32).reshape(2, 4, 2, 8, 512)
    send(S.at[:, :, 1 - c], Sc, s_st.at[0], r_sc.at[0], sibling)

    k_spread = (z // 8) * 4 + ((z % 8) // 4) * 2 + y % 2

    def hid_at(k):
        return hid.at[pl.ds(pl.multiple_of(k * 32, 32), 32), :]

    @pl.when(is_spread)
    def _():
        each(0, 8, lambda i: done(hx.at[i], r_h1.at[i]))
        r, s = iota((128, 128), 0), iota((128, 128), 1)
        perm = ((s >> 4) == (r & 7)) & (((s >> 2) & 3) == (r >> 5)) & ((s & 3) == ((r >> 3) & 3))
        rows = jnp.dot(
            jnp.where(perm, 1.0, 0.0).astype(BF16), hx[...].reshape(128, 512), preferred_element_type=F32
        ).astype(BF16)
        for q in range(4):
            hid[pl.ds(pl.multiple_of(k_spread * 32, 32), 32), pl.ds(q * 512, 512)] = rows[q * 32:(q + 1) * 32]
        each(1, 16, lambda d: send(
            hid_at(k_spread), hid_at(k_spread), s_h2.at[d], r_h2.at[k_spread], z_to(d)))

    for half, d in ((0, 4), (1, 12)):
        zd = (z + d) % 16
        p = piece(1 - zd // 8, x, c, half)
        done(relay.at[half], r_relay.at[half])
        send(relay.at[half], w_at(p), s_rf.at[half], r_w.at[p], dev(zd, xc, y))

    def ring(zg):
        left, right, far = (x + 3) % 4, (x + 1) % 4, (x + 2) % 4
        for half in range(2):
            near, turn = (left, 1) if half == 0 else (right, 3)
            p = piece(zg, near, c, half)
            done(w_at(p), r_w.at[p])
            send(w_at(p), w_at(p), s_xf.at[zg * 2 + half], r_w.at[p], x_to(turn))
            send(w_at(p), w_at(p), s_c.at[p], r_w.at[p], sibling)
        for half in range(2):
            near = right if half == 0 else left
            p = piece(zg, near, c, half)
            done(w_at(p), r_w.at[p])
            send(w_at(p), w_at(p), s_c.at[p], r_w.at[p], sibling)
        for half in range(2):
            p = piece(zg, far, c, half)
            done(w_at(p), r_w.at[p])
            send(w_at(p), w_at(p), s_c.at[p], r_w.at[p], sibling)

    @pl.when(y // 2 == c)
    def _():
        def go(k4):
            k = k4 * 2 + y % 2

            @pl.when(jnp.logical_not(jnp.logical_and(is_spread, k == k_spread)))
            def _():
                done(hid_at(k), r_h2.at[k])

            each(1, 4, lambda d: send(hid_at(k), hid_at(k), s_h3.at[k4 * 3 + d - 1], r_h2.at[k], y_to(d)))
        each(0, 4, go)

    done(Sc, r_sc.at[0])
    for h in range(2):
        for x_ in range(4):
            A[x_, h] = S[h, x_, c] + Sc[h, x_]
    each(1, 4, lambda d: send(A.at[(x + d) % 4], Sx.at[x], s_st.at[d], r_sx.at[x], x_to(d)))

    ring(zh)

    each(1, 4, lambda d: done(Sx.at[(x + d) % 4], r_sx.at[(x + d) % 4]))
    total = A[x] + Sx[(x + 1) % 4] + Sx[(x + 2) % 4] + Sx[(x + 3) % 4]
    T[0] = total[:, :, :1024]
    T[1] = total[:, :, 1024:]
    send(T.at[1 - zh], Sz, s_st.at[4], r_sz.at[0], partner)

    for half in range(2):
        p = piece(1 - zh, x, c, half)
        done(w_at(p), r_w.at[p])
        send(w_at(p), w_at(p), s_xl.at[4 + half * 2], r_w.at[p], x_to(1))
        send(w_at(p), w_at(p), s_xl.at[5 + half * 2], r_w.at[p], x_to(3))
        send(w_at(p), w_at(p), s_c.at[p], r_w.at[p], sibling)
    ring(1 - zh)

    def last_hidden(k):
        @pl.when(jnp.logical_not(jnp.logical_and(y // 2 == c, y % 2 == k % 2)))
        def _():
            done(hid_at(k), r_h2.at[k])
    each(0, 8, last_hidden)

    done(Sz, r_sz.at[0])
    student = (T[zh] + Sz[...]).reshape(16, 1024)
    SL[...] = student
    s_top = jnp.max(student, axis=1, keepdims=True)
    s_sum = jnp.sum(jnp.exp(student - s_top), axis=1, keepdims=True)
    mine_tok = row_token(iota((16, 128), 1)) == iota((16, 128), 0)
    s_top = jnp.sum(jnp.where(mine_tok, s_top, 0.0), axis=0, keepdims=True)
    s_sum = jnp.sum(jnp.where(mine_tok, s_sum, 0.0), axis=0, keepdims=True)

    def from_sibling(i):
        p = (i // 2) * 4 + (1 - c) * 2 + i % 2
        done(w_at(p), r_w.at[p])
    each(0, 16, from_sibling)
    for half in range(2):
        p = piece(zh, x, c, half)
        pltpu.make_async_copy(head.at[pl.ds(half * 64, 64), mine], w_at(p), l_w.at[half]).wait()

    def scores(n):
        cols = pl.ds(pl.multiple_of(n * 256, 256), 256)
        L[:, cols] = jnp.dot(hid[...], W[:, cols], preferred_element_type=F32)
    each(0, 4, scores)

    def local_stats(n):
        rows = pl.ds(pl.multiple_of(n * 32, 32), 32)
        logits = L[rows, :]
        top = jnp.max(logits, axis=1, keepdims=True)
        low = logits - top
        e = jnp.exp(low)
        Eb[rows, :] = e.astype(BF16)
        Cb[rows, :] = low.astype(BF16)
        mbuf[rows, :] = jnp.broadcast_to(top, (32, 128))
        sbuf[rows, :] = jnp.broadcast_to(jnp.sum(e, axis=1, keepdims=True), (32, 128))
    each(0, 8, local_stats)

    cross = fold_tokens(lax.dot_general(
        Eb[...], Cb[...], (((1,), (1,)), ((), ())), preferred_element_type=F32))
    tops = mbuf[...]
    tops = fold_tokens(jnp.concatenate([tops, tops], axis=1))
    sums = sbuf[...]
    sums = fold_tokens(jnp.concatenate([sums, sums], axis=1))
    local_top = own_lane(tops)
    cross = cross + sums * local_top
    yb[y, 0:2] = cross.reshape(2, 8, 256)
    yb[y, 2:4] = tops.reshape(2, 8, 256)
    yb[y, 4:6] = sums.reshape(2, 8, 256)
    yb[y, 6] = jnp.broadcast_to(jnp.concatenate([s_top, s_sum], axis=1), (8, 256))
    each(1, 4, lambda d: send(yb.at[y], yb.at[y], s_y.at[d], r_y.at[y], y_to(d)))
    each(1, 4, lambda d: done(yb.at[(y + d) % 4], r_y.at[(y + d) % 4]))
    got = yb[...]
    y_top = jnp.max(got[:, 2:4], axis=0)
    y_scale = jnp.exp(got[:, 2:4] - y_top[None])
    xb[:, 0, :] = jnp.sum(got[:, 0:2] * y_scale, axis=0).reshape(16, 256)
    xb[:, 1, :] = y_top.reshape(16, 256)
    xb[:, 2, :] = jnp.sum(got[:, 4:6] * y_scale, axis=0).reshape(16, 256)
    y_stop = jnp.max(got[:, 6, :, :128], axis=0)
    y_ssum = jnp.sum(got[:, 6, :, 128:] * jnp.exp(got[:, 6, :, :128] - y_stop[None]), axis=0)
    s_row = jnp.concatenate([y_stop, y_ssum], axis=1)
    xb[:, 3, :] = jnp.concatenate([s_row, s_row], axis=0)

    each(1, 16, lambda d: send(xb.at[(z + d) % 16], rb.at[z], s_z1.at[d], r_z1.at[z], z_to(d)))
    rb[pl.ds(z, 1)] = xb[pl.ds(z, 1)]
    each(1, 16, lambda d: done(rb.at[(z + d) % 16], r_z1.at[(z + d) % 16]))
    z_tops = rb[:, 1, :]
    z_top = jnp.max(z_tops, axis=0, keepdims=True)
    z_scale = jnp.exp(z_tops - z_top)
    z_sum = jnp.sum(rb[:, 2, :] * z_scale, axis=0, keepdims=True)
    z_cross = jnp.sum(rb[:, 0, :] * z_scale, axis=0, keepdims=True) / z_sum
    stud = rb[:, 3, :]
    stud_top = jnp.max(stud[:, :128], axis=0, keepdims=True)
    stud_sum = jnp.sum(stud[:, 128:] * jnp.exp(stud[:, :128] - stud_top), axis=0, keepdims=True)
    stud_norm = stud_top + jnp.log(stud_sum)
    gb[pl.ds(z, 1)] = jnp.concatenate([z_cross, z_top + jnp.log(z_sum)], axis=0)[None]
    each(1, 16, lambda d: send(gb.at[z], gb.at[z], s_z2.at[d], r_z2.at[z], z_to(d)))
    each(1, 16, lambda d: done(gb.at[(z + d) % 16], r_z2.at[(z + d) % 16]))
    norm = own_lane(gb[:, 1, :])
    ce = norm - gb[:, 0, :]
    ce_out[...] = ce
    inverse = 1.0 / (1.0 + jnp.sum(ce, axis=0, keepdims=True) / 16.0)
    r, l = iota((256, 256), 0), iota((256, 256), 1)
    by_row = jnp.sum(jnp.where(r == l, inverse, 0.0), axis=1, keepdims=True)
    share = jnp.sum(jnp.where(row_token(r) == row_token(l), by_row, 0.0), axis=0, keepdims=True)
    weights = inverse / share
    agree_out[...] = jnp.broadcast_to(weights * 16.0, (8, 256))
    scale = weights * jnp.exp(local_top - norm)
    spread_w = jnp.where(iota((16, 256), 0) == row_token(iota((16, 256), 1)), scale, 0.0)
    coarse = spread_w.astype(BF16)
    fine = (spread_w - coarse.astype(F32)).astype(BF16)
    soft = jnp.dot(coarse, Eb[...], preferred_element_type=F32) + jnp.dot(fine, Eb[...], preferred_element_type=F32)

    done(lab.at[1 - zh], r_lab.at[0])
    lane = iota((16, 128), 1)
    first = (row_token(lane) == iota((16, 128), 0)) & ((lane & 7) == 0)
    s_norm = jnp.sum(jnp.where(first, stud_norm, 0.0), axis=1, keepdims=True)
    ids = lab[...].reshape(16, 128)
    ids = jnp.concatenate([ids] * 8, axis=1)
    onehot = jnp.where(iota((16, 1024), 1) + (v * 2048 + zh * 1024) == ids, HARD_SHARE, 0.0)
    residual = jnp.exp(SL[...] - s_norm) - ((1.0 - HARD_SHARE) * soft + onehot)
    R[zh, xc] = residual.astype(BF16)

    send(R.at[zh, xc], R.at[zh, xc], s_r.at[0], r_r.at[zh * 8 + xc], partner)

    def spread_r(zg, base):
        each(1, 8, lambda d: send(R.at[zg, xc], R.at[zg, xc], s_r.at[base + d], r_r.at[zg * 8 + xc], xc_to(d)))
    spread_r(zh, 0)
    done(R.at[1 - zh, xc], r_r.at[(1 - zh) * 8 + xc])
    spread_r(1 - zh, 7)
    tokens = sh[...].astype(F32).reshape(2, 8, 8, 128)
    tokens = jnp.swapaxes(tokens, 0, 1).reshape(128, 128).astype(BF16)
    for f in range(2):
        each(1, 8, lambda d: done(R.at[f, (xc + d) % 8], r_r.at[f * 8 + (xc + d) % 8]))
        for k in range(2):
            grad_out[:, pl.ds(f * 1024 + k * 512, 512)] = lax.dot_general(
                tokens, R[f, :, :, pl.ds(k * 512, 512)].reshape(128, 512),
                (((0,), (0,)), ((), ())), preferred_element_type=F32)

    for half in range(2):
        done(relay.at[half], s_z.at[half])
        done(relay.at[half], s_rf.at[half])
    for i in range(8):
        done(w_at(0), s_xl.at[i])
    for i in range(4):
        done(w_at(0), s_xf.at[i])

    def own_core(i):
        p = (i // 2) * 4 + c * 2 + i % 2
        done(w_at(p), s_c.at[p])
    each(0, 16, own_core)

    @pl.when(jnp.logical_not(is_spread))
    def _():
        done(hx.at[0], s_h1.at[0])

    @pl.when(is_spread)
    def _():
        each(1, 16, lambda d: done(hid_at(0), s_h2.at[d]))

    @pl.when(y // 2 == c)
    def _():
        each(0, 12, lambda i: done(hid_at(0), s_h3.at[i]))
    done(Sc, s_st.at[0])
    each(1, 4, lambda d: done(A.at[0], s_st.at[d]))
    done(Sz, s_st.at[4])
    done(lab.at[0], s_st.at[5])
    each(1, 4, lambda d: done(yb.at[0], s_y.at[d]))
    each(1, 16, lambda d: done(rb.at[0], s_z1.at[d]))
    each(1, 16, lambda d: done(gb.at[0], s_z2.at[d]))
    each(0, 15, lambda i: done(R.at[0, 0], s_r.at[i]))


def on_device(teacher_hidden, teacher_head, student_hidden, student_head, labels):
    hid = teacher_hidden[0].reshape(4, 4, 512).transpose(1, 0, 2).reshape(16, 512)
    lab = jnp.broadcast_to(labels[:, None], (8, 128))
    vmem = lambda shape, dtype=F32: pltpu.VMEM(shape, dtype)
    dma = lambda n: pltpu.SemaphoreType.DMA((n,))
    space = pl.BlockSpec(memory_space=pltpu.VMEM)
    grad, ce, agree = pl.pallas_call(
        kernel,
        out_shape=(
            jax.ShapeDtypeStruct((128, 2048), F32),
            jax.ShapeDtypeStruct((16, 256), F32),
            jax.ShapeDtypeStruct((8, 256), F32),
        ),
        in_specs=[space] * 5,
        out_specs=(space,) * 3,
        scratch_shapes=[
            vmem((2048, 1024), BF16), vmem((2, 64, 1024), BF16), vmem((8, 16, 512), BF16), vmem((256, 2048), BF16),
            vmem((256, 1024)), vmem((256, 1024), BF16), vmem((256, 1024), BF16), vmem((256, 128)), vmem((256, 128)),
            vmem((2, 4, 2, 8, 2048)), vmem((2, 4, 8, 2048)), vmem((4, 2, 8, 2048)), vmem((4, 2, 8, 2048)),
            vmem((2, 2, 8, 1024)), vmem((2, 8, 1024)), vmem((16, 1024)), vmem((2, 8, 128), I32),
            vmem((4, 7, 8, 256)), vmem((16, 4, 256)), vmem((16, 4, 256)), vmem((16, 2, 256)),
            vmem((2, 8, 16, 1024), BF16),
            dma(2), dma(2), dma(8), dma(4), dma(32), dma(1), dma(16), dma(12), dma(6), dma(4), dma(16), dma(16), dma(15),
            dma(2), dma(32), dma(8), dma(8), dma(1), dma(4), dma(1), dma(1), dma(4), dma(16), dma(16), dma(16), dma(2),
        ],
        compiler_params=pltpu.CompilerParams(
            collective_id=0, has_side_effects=True, vmem_limit_bytes=48 << 20
        ),
    )(hid, teacher_head, student_hidden, student_head, lab)
    z_hi = lax.axis_index("teacher") // 8
    ce = lax.dynamic_slice_in_dim(ce.reshape(16, 2, 16, 8), 8 * z_hi, 8, 2)
    agree = lax.dynamic_slice_in_dim(agree[0].reshape(2, 16, 8), 8 * z_hi, 8, 1)
    return (
        ce.transpose(2, 0, 1, 3).reshape(8, 16, 16),
        agree.transpose(1, 0, 2).reshape(8, 16),
        grad,
    )


def solution(mesh):
    return jax.shard_map(
        on_device,
        mesh=mesh,
        in_specs=(
            P("teacher", "vocab", None),
            P("teacher", "vocab"),
            P(None, "teacher"),
            P("teacher", "vocab"),
            P("teacher"),
        ),
        out_specs=(P("teacher", None, None), P("teacher", None), P("teacher", "vocab")),
        check_vma=False,
    )
```

time: 844 us -> 126 us (0.15)
  blocking collectives: 587 us -> 0 us
  waiting for transfers between devices: 186 us -> 0 us
  Pallas kernels: 0 us -> 120 us
  starting transfers between devices: 34.6 us -> 0 us
  between operations: 14.2 us -> 0.71 us
    psum x2 -> x0, blocking collectives: 300 us -> none  [the longest x1 196 us: on_device(): cross_matrix = lax.psum(cross_local, 'vocab')]
    all_gather x2 -> x0, blocking collectives: 187 us -> none  [the longest x1 123 us: on_device(): gathered = lax.all_gather(teacher_hidden, 'vocab', axis=1, tiled=True)]
    all_gather x1 -> x0, waiting for transfers between devices: 167 us -> none  [on_device(): lax.all_gather(teacher_head, 'teacher', axis=0, tiled=True)]
    pallas_call x0 -> x1, Pallas kernels: none -> 120 us  [on_device(): pl.pallas_call(kernel, out_shape=(jax.ShapeDtypeStruct((128, 2048), F32),...]
    pmax x1 -> x0, blocking collectives: 100 us -> none  [teacher_normalizer(): highest = lax.pmax(jnp.max(logits, axis=1), 'vocab')]
    all_to_all x1 -> x0, starting transfers between devices: 34.5 us -> none  [on_device(): lax.all_to_all(log_prob[None], 'teacher', split_axis=1, concat_axis=0, ti...]
    all_to_all x1 -> x0, waiting for transfers between devices: 18.3 us -> none  [on_device(): lax.all_to_all(log_prob[None], 'teacher', split_axis=1, concat_axis=0, ti...]
  transfers between devices with their start and end apart: 3 -> 0, of which waited for: 2 -> 0; matrix products, arithmetic and copies ran while one was open for 0% -> 0% of each run, Pallas kernels for 0% -> 0%
where the time goes in v1:
time: 126 us
  Pallas kernels  120 us (95%)
  local copies, waits for them, and re-layouts  5.41 us (4%)
    pallas_call x1, Pallas kernels, on_device(): pl.pallas_call(kernel, out_shape=(jax.ShapeDtypeStruct((128, 2048), F32),...  120 us
    unnamed x12, local copies, waits for them, and re-layouts  4.44 us

profile of v1, /device:TPU:1, one launch (start us, length us, event | category | flops | bytes accessed | tf_op | source)
XLA Modules:
  0.0 125.9 jit_solution(15690450499060095372)
XLA Ops:
  0.6 0.0 copy-start.4
  0.6 0.0 copy-start.3
  0.7 0.0 copy-start.2
  0.7 0.6 copy-done.4
  1.3 0.1 broadcast_in_dim.2.lab_in
  1.4 0.0 copy-done.3
  1.4 0.0 copy-done.2
  1.4 0.0 copy-start
  1.4 1.0 copy-done
  2.5 0.0 copy-start.1
  2.5 1.0 copy-done.1
  3.5 119.8 %shard_map.76 = (f32[128,2048]{1,0:T(8,128)S(1)}, f32[16,256]{1,0:T(8,128)S(1)}, f32[8,256]{1,0:T(8,128)S(1)}) custom-call(bf16[16,512]{1,0:T(8,128)(2,1)S(1)} %reshape.19.hid_in, bf16[128,2048]{1,0:T(8,128)(2,1)S(1)} %copy-done, bf16[128,128]{1,0:T(8,128)(2,1)S(1)} %copy-done.2, bf16[128,2048]{1,0:T(8,128)(2,1)S(1)} %copy-done.1, ...), custom_call_target="tpu_custom_call" | custom-call | tf_op jit(solution)/shard_map/pallas_call | solution.py:354
  123.3 0.1 reshape_squeeze.7
  123.4 0.7 reshape.22
  124.1 0.1 copy.12
  124.2 0.7 copy.15
  124.9 1.0 copy.18
  (5 shorter events, 0.0 us)
Async XLA Ops:
  0.6 0.7 copy-start.4
  0.6 0.7 copy-start.3
  0.7 0.8 copy-start.2
  1.4 1.0 copy-start
  2.5 1.0 copy-start.1

commit v2 on v1

v2 whole, which is shorter than its diff:
```python
import jax
import jax.numpy as jnp
from jax import lax
from jax.experimental import pallas as pl
from jax.experimental.pallas import tpu as pltpu
from jax.sharding import PartitionSpec as P

HARD_SHARE = 0.3
MESH = pl.DeviceIdType.MESH
F32 = jnp.float32
BF16 = jnp.bfloat16
I32 = jnp.int32
PARTS = 2
ROWS = 128 // PARTS


def iota(shape, dim):
    return lax.broadcasted_iota(I32, shape, dim)


def row_token(r):
    return (r >> 3) & 15


def row_teacher(r):
    return (r >> 7) * 8 + (r & 7)


def fold_tokens(values):
    same = row_token(iota((256, 256), 0)) == row_token(iota((256, 256), 1))
    kept = jnp.where(same, values, 0.0).reshape(2, 16, 8, 256)
    return jnp.sum(kept, axis=1).reshape(16, 256)


def own_lane(values):
    same = iota((16, 256), 0) == row_teacher(iota((16, 256), 1))
    return jnp.sum(jnp.where(same, values, 0.0), axis=0, keepdims=True)


def kernel(
    hid_in, head, sh, shead_in, lab_in,
    grad_out, ce_out, agree_out,
    shead, W, hx, hid, L, Eb, Cb, mbuf, sbuf,
    S, Sc, A, Sx, T, Sz, SL, lab, yb, ys, xb, rb, gb, R,
    s_z, s_x, s_c, s_h1, s_h2, s_h3, s_st, s_y, s_ys, s_z1, s_z2, s_r,
    r_w, r_h1, r_h2, r_sc, r_sx, r_sz, r_lab, r_y, r_ys, r_z1, r_z2, r_r, l_w, l_in,
):
    t = lax.axis_index("teacher")
    v = lax.axis_index("vocab")
    zh, xc = t // 8, t % 8
    x, c = xc // 2, xc % 2
    zl, y = v // 4, v % 4
    z = zh * 8 + zl

    def dev(z_, xc_, y_):
        return {"teacher": (z_ // 8) * 8 + xc_, "vocab": (z_ % 8) * 4 + y_}

    def send(src, dst, ssem, rsem, to):
        pltpu.make_async_remote_copy(
            src_ref=src, dst_ref=dst, send_sem=ssem, recv_sem=rsem, device_id=to, device_id_type=MESH
        ).start()

    def done(ref, sem):
        pltpu.make_async_copy(ref, ref, sem).wait()

    def each(lo, hi, body):
        def step(i, carry):
            body(i)
            return carry
        lax.fori_loop(lo, hi, step, 0)

    z_to = lambda d: dev((z + d) % 16, xc, y)
    x_to = lambda d: dev(z, ((x + d) % 4) * 2 + c, y)
    y_to = lambda d: dev(z, xc, (y + d) % 4)
    xc_to = lambda d: dev(z, (xc + d) % 8, y)
    sibling = dev(z, x * 2 + 1 - c, y)
    partner = z_to(8)

    pltpu.make_async_copy(shead_in, shead, l_in.at[0]).start()
    barrier = pltpu.get_barrier_semaphore()
    each(1, 16, lambda d: pl.semaphore_signal(barrier, inc=1, device_id=z_to(d), device_id_type=MESH))
    each(1, 8, lambda d: pl.semaphore_signal(barrier, inc=1, device_id=xc_to(d), device_id_type=MESH))
    each(1, 4, lambda d: pl.semaphore_signal(barrier, inc=1, device_id=y_to(d), device_id_type=MESH))

    mine = pl.ds(pl.multiple_of(zh * 1024, 1024), 1024)
    other = pl.ds(pl.multiple_of((1 - zh) * 1024, 1024), 1024)
    piece = lambda zh_, x_, c_, part: ((zh_ * 8 + x_ * 2 + c_) * PARTS) + part
    w_at = lambda p: W.at[pl.ds(pl.multiple_of(p * ROWS, ROWS), ROWS), :]
    block = W.at[pl.ds(pl.multiple_of(t * 128, 128), 128), :]
    pltpu.make_async_copy(head.at[:, mine], block, l_w.at[0]).start()
    pltpu.make_async_copy(shead_in, shead, l_in.at[0]).wait()
    for k in range(4):
        cols = pl.ds(k * 512, 512)
        S[:, :, :, :, cols] = jnp.dot(sh[...], shead[:, cols], preferred_element_type=F32).reshape(2, 4, 2, 8, 512)
    lab[pl.ds(zh, 1)] = lab_in[...][None]
    pltpu.make_async_copy(head.at[:, mine], block, l_w.at[0]).wait()
    pl.semaphore_wait(barrier, 25)

    spread = (z % 4) * 2 + y // 2
    is_spread = xc == spread
    to_spread = dev(z, spread, y)

    @pl.when(is_spread)
    def _():
        pltpu.make_async_copy(hid_in, hx.at[xc], r_h1.at[xc]).start()

    @pl.when(jnp.logical_not(is_spread))
    def _():
        send(hid_in, hx.at[xc], s_h1.at[0], r_h1.at[xc], to_spread)

    carries = y // 2 == c

    def to_partner(part):
        p = piece(zh, x, c, part)
        send(head.at[pl.ds(pl.multiple_of(part * ROWS, ROWS), ROWS), other], w_at(p), s_z.at[part], r_w.at[p], partner)

    def along_x(zg, part):
        p = piece(zg, x, c, part)
        each(1, 4, lambda d: send(w_at(p), w_at(p), s_x.at[(zg * PARTS + part) * 3 + d - 1], r_w.at[p], x_to(d)))
        send(w_at(p), w_at(p), s_c.at[p], r_w.at[p], sibling)

    def from_x(zg):
        def go(i):
            p = piece(zg, (x + 1 + (i % 3) * 2 % 3) % 4, c, i // 3)
            done(w_at(p), r_w.at[p])
            send(w_at(p), w_at(p), s_c.at[p], r_w.at[p], sibling)
        each(0, 3 * PARTS, go)

    @pl.when(jnp.logical_not(carries))
    def _():
        each(0, PARTS, to_partner)
    each(0, PARTS, lambda part: along_x(zh, part))
    send(S.at[:, :, 1 - c], Sc, s_st.at[0], r_sc.at[0], sibling)

    k_spread = (z // 8) * 4 + ((z % 8) // 4) * 2 + y % 2

    def hid_at(k):
        return hid.at[pl.ds(pl.multiple_of(k * 32, 32), 32), :]

    @pl.when(is_spread)
    def _():
        each(0, 8, lambda i: done(hx.at[i], r_h1.at[i]))
        r, s = iota((128, 128), 0), iota((128, 128), 1)
        perm = ((s >> 4) == (r & 7)) & (((s >> 2) & 3) == (r >> 5)) & ((s & 3) == ((r >> 3) & 3))
        rows = jnp.dot(
            jnp.where(perm, 1.0, 0.0).astype(BF16), hx[...].reshape(128, 512), preferred_element_type=F32
        ).astype(BF16)
        for q in range(4):
            hid[pl.ds(pl.multiple_of(k_spread * 32, 32), 32), pl.ds(q * 512, 512)] = rows[q * 32:(q + 1) * 32]
        def go(i):
            d = (1 - i % 2) * (i // 2 + 1) + (i % 2) * (15 - i // 2)
            send(hid_at(k_spread), hid_at(k_spread), s_h2.at[i], r_h2.at[k_spread], z_to(d))
        each(0, 15, go)

    done(Sc, r_sc.at[0])
    for h in range(2):
        for x_ in range(4):
            A[x_, h] = S[h, x_, c] + Sc[h, x_]

    from_x(zh)
    each(1, 4, lambda d: send(A.at[(x + d) % 4], Sx.at[x], s_st.at[d], r_sx.at[x], x_to(d)))

    @pl.when(carries)
    def _():
        def go(k4):
            k = k4 * 2 + y % 2

            @pl.when(jnp.logical_not(jnp.logical_and(is_spread, k == k_spread)))
            def _():
                done(hid_at(k), r_h2.at[k])

            each(1, 4, lambda d: send(hid_at(k), hid_at(k), s_h3.at[k4 * 3 + d - 1], r_h2.at[k], y_to(d)))
        each(0, 4, go)
        each(0, PARTS, to_partner)

    each(1, 4, lambda d: done(Sx.at[(x + d) % 4], r_sx.at[(x + d) % 4]))
    total = A[x] + Sx[(x + 1) % 4] + Sx[(x + 2) % 4] + Sx[(x + 3) % 4]
    T[0] = total[:, :, :1024]
    T[1] = total[:, :, 1024:]

    def from_partner(part):
        p = piece(1 - zh, x, c, part)
        done(w_at(p), r_w.at[p])
        along_x(1 - zh, part)
    each(0, PARTS, from_partner)
    from_x(1 - zh)

    def last_hidden(k):
        @pl.when(jnp.logical_not(jnp.logical_and(y // 2 == c, y % 2 == k % 2)))
        def _():
            done(hid_at(k), r_h2.at[k])
    each(0, 8, last_hidden)

    def from_sibling(i):
        p = (i // PARTS) * (2 * PARTS) + (1 - c) * PARTS + i % PARTS
        done(w_at(p), r_w.at[p])
    each(0, 8 * PARTS, from_sibling)
    send(T.at[1 - zh], Sz, s_st.at[4], r_sz.at[0], partner)
    send(lab.at[zh], lab.at[zh], s_st.at[5], r_lab.at[0], partner)

    def scores(n):
        cols = pl.ds(pl.multiple_of(n * 256, 256), 256)
        L[:, cols] = jnp.dot(hid[...], W[:, cols], preferred_element_type=F32)
    each(0, 4, scores)

    def local_stats(n):
        rows = pl.ds(pl.multiple_of(n * 32, 32), 32)
        logits = L[rows, :]
        top = jnp.max(logits, axis=1, keepdims=True)
        low = logits - top
        e = jnp.exp(low)
        Eb[rows, :] = e.astype(BF16)
        Cb[rows, :] = low.astype(BF16)
        mbuf[rows, :] = jnp.broadcast_to(top, (32, 128))
        sbuf[rows, :] = jnp.broadcast_to(jnp.sum(e, axis=1, keepdims=True), (32, 128))
    each(0, 8, local_stats)

    cross = fold_tokens(lax.dot_general(
        Eb[...], Cb[...], (((1,), (1,)), ((), ())), preferred_element_type=F32))
    tops = mbuf[...]
    tops = fold_tokens(jnp.concatenate([tops, tops], axis=1))
    sums = sbuf[...]
    sums = fold_tokens(jnp.concatenate([sums, sums], axis=1))
    local_top = own_lane(tops)
    cross = cross + sums * local_top
    yb[y, 0:2] = cross.reshape(2, 8, 256)
    yb[y, 2:4] = jnp.concatenate([tops[:, :128], sums[:, 128:]], axis=1).reshape(2, 8, 256)
    each(1, 4, lambda d: send(yb.at[y], yb.at[y], s_y.at[d], r_y.at[y], y_to(d)))

    done(Sz, r_sz.at[0])
    student = (T[zh] + Sz[...]).reshape(16, 1024)
    SL[...] = student
    s_top = jnp.max(student, axis=1, keepdims=True)
    s_sum = jnp.sum(jnp.exp(student - s_top), axis=1, keepdims=True)
    mine_tok = row_token(iota((16, 128), 1)) == iota((16, 128), 0)
    s_top = jnp.sum(jnp.where(mine_tok, s_top, 0.0), axis=0, keepdims=True)
    s_sum = jnp.sum(jnp.where(mine_tok, s_sum, 0.0), axis=0, keepdims=True)
    ys[pl.ds(y, 1)] = jnp.concatenate([s_top, s_sum], axis=0)[None]
    each(1, 4, lambda d: send(ys.at[y], ys.at[y], s_ys.at[d], r_ys.at[y], y_to(d)))

    each(1, 4, lambda d: done(yb.at[(y + d) % 4], r_y.at[(y + d) % 4]))
    twice = lambda a: jnp.concatenate([a, a], axis=-1)
    got = yb[...]
    y_top = jnp.max(got[:, 2:4, :, :128], axis=0)
    y_scale = jnp.exp(got[:, 2:4, :, :128] - y_top[None])
    y_sum = jnp.sum(got[:, 2:4, :, 128:] * y_scale, axis=0)
    xb[:, 0, :] = jnp.sum(got[:, 0:2] * twice(y_scale), axis=0).reshape(16, 256)
    xb[:, 1, :] = jnp.concatenate([y_top, y_sum], axis=-1).reshape(16, 256)

    each(1, 16, lambda d: send(xb.at[(z + d) % 16], rb.at[z], s_z1.at[d], r_z1.at[z], z_to(d)))
    rb[pl.ds(z, 1)] = xb[pl.ds(z, 1)]
    each(1, 4, lambda d: done(ys.at[(y + d) % 4], r_ys.at[(y + d) % 4]))
    ytops, ysums = ys[:, 0, :], ys[:, 1, :]
    s_top = jnp.max(ytops, axis=0, keepdims=True)
    s_sum = jnp.sum(ysums * jnp.exp(ytops - s_top), axis=0, keepdims=True)
    each(1, 16, lambda d: done(rb.at[(z + d) % 16], r_z1.at[(z + d) % 16]))
    z_tops = rb[:, 1, :128]
    z_top = jnp.max(z_tops, axis=0, keepdims=True)
    z_scale = jnp.exp(z_tops - z_top)
    z_sum = jnp.sum(rb[:, 1, 128:] * z_scale, axis=0, keepdims=True)
    z_cross = jnp.sum(rb[:, 0, :] * twice(z_scale), axis=0, keepdims=True) / twice(z_sum)
    lane = iota((1, 256), 1)
    stud = jnp.where((lane & 1) == 0, twice(s_top), twice(s_sum))
    z_norm = jnp.where((lane >> 7) == z // 8, twice(z_top + jnp.log(z_sum)), stud)
    gb[pl.ds(z, 1)] = jnp.concatenate([z_cross, z_norm], axis=0)[None]
    each(1, 16, lambda d: send(gb.at[z], gb.at[z], s_z2.at[d], r_z2.at[z], z_to(d)))
    each(1, 16, lambda d: done(gb.at[(z + d) % 16], r_z2.at[(z + d) % 16]))
    norms = gb[:, 1, :]
    norm = own_lane(norms)
    ce = norm - gb[:, 0, :]
    ce_out[...] = ce
    inverse = 1.0 / (1.0 + jnp.sum(ce, axis=0, keepdims=True) / 16.0)
    r, l = iota((256, 256), 0), iota((256, 256), 1)
    by_row = jnp.sum(jnp.where(r == l, inverse, 0.0), axis=1, keepdims=True)
    share = jnp.sum(jnp.where(row_token(r) == row_token(l), by_row, 0.0), axis=0, keepdims=True)
    weights = inverse / share
    agree_out[...] = jnp.broadcast_to(weights * 16.0, (8, 256))
    scale = weights * jnp.exp(local_top - norm)
    spread_w = jnp.where(iota((16, 256), 0) == row_token(iota((16, 256), 1)), scale, 0.0)
    coarse = spread_w.astype(BF16)
    fine = (spread_w - coarse.astype(F32)).astype(BF16)
    soft = jnp.dot(coarse, Eb[...], preferred_element_type=F32) + jnp.dot(fine, Eb[...], preferred_element_type=F32)

    stud = jnp.concatenate([norms[:8, 128:], norms[8:, :128]], axis=0)
    stud_top = jnp.max(stud, axis=0, keepdims=True)
    stud_sums = pltpu.roll(stud, 127, 1)
    even = (iota((16, 128), 1) & 1) == 0
    stud_top = jnp.max(jnp.where(even, stud, -jnp.inf), axis=0, keepdims=True)
    stud_top = jnp.where(even[:1], stud_top, 0.0)
    stud_sum = jnp.sum(jnp.where(even, stud_sums * jnp.exp(jnp.where(even, stud - stud_top, 0.0)), 1.0), axis=0, keepdims=True)
    stud_norm = stud_top + jnp.log(stud_sum)

    done(lab.at[1 - zh], r_lab.at[0])
    lane = iota((16, 128), 1)
    first = (row_token(lane) == iota((16, 128), 0)) & ((lane & 7) == 0)
    s_norm = jnp.sum(jnp.where(first, stud_norm, 0.0), axis=1, keepdims=True)
    ids = lab[...].reshape(16, 128)
    ids = jnp.concatenate([ids] * 8, axis=1)
    onehot = jnp.where(iota((16, 1024), 1) + (v * 2048 + zh * 1024) == ids, HARD_SHARE, 0.0)
    residual = jnp.exp(SL[...] - s_norm) - ((1.0 - HARD_SHARE) * soft + onehot)
    R[zh, xc] = residual.astype(BF16)

    def pass_r(f, xc_, i, to):
        send(R.at[f, xc_], R.at[f, xc_], s_r.at[i], r_r.at[f * 8 + xc_], to)

    def await_r(f, xc_):
        done(R.at[f, xc_], r_r.at[f * 8 + xc_])

    pass_r(zh, xc, 0, partner)
    each(1, 4, lambda d: pass_r(zh, xc, d, x_to(d)))
    pass_r(zh, xc, 4, sibling)

    def relay_r(f, base):
        def go(d):
            xc_ = ((x + d) % 4) * 2 + c
            await_r(f, xc_)
            pass_r(f, xc_, base + d, sibling)
        each(1, 4, go)

    relay_r(zh, 4)
    tokens = sh[...].astype(F32).reshape(2, 8, 8, 128)
    tokens = jnp.swapaxes(tokens, 0, 1).reshape(128, 128).astype(BF16)
    await_r(1 - zh, xc)
    each(1, 4, lambda d: pass_r(1 - zh, xc, 7 + d, x_to(d)))
    pass_r(1 - zh, xc, 11, sibling)
    relay_r(1 - zh, 11)
    for f in range(2):
        each(0, 4, lambda i: await_r(f, i * 2 + 1 - c))
    for f in range(2):
        for k in range(2):
            grad_out[:, pl.ds(f * 1024 + k * 512, 512)] = lax.dot_general(
                tokens, R[f, :, :, pl.ds(k * 512, 512)].reshape(128, 512),
                (((0,), (0,)), ((), ())), preferred_element_type=F32)

    each(0, PARTS, lambda i: done(w_at(0), s_z.at[i]))
    each(0, 6 * PARTS, lambda i: done(w_at(0), s_x.at[i]))

    def own_core(i):
        p = (i // PARTS) * (2 * PARTS) + c * PARTS + i % PARTS
        done(w_at(p), s_c.at[p])
    each(0, 8 * PARTS, own_core)

    @pl.when(jnp.logical_not(is_spread))
    def _():
        done(hx.at[0], s_h1.at[0])

    @pl.when(is_spread)
    def _():
        each(0, 15, lambda d: done(hid_at(0), s_h2.at[d]))

    @pl.when(y // 2 == c)
    def _():
        each(0, 12, lambda i: done(hid_at(0), s_h3.at[i]))
    done(Sc, s_st.at[0])
    each(1, 4, lambda d: done(A.at[0], s_st.at[d]))
    done(Sz, s_st.at[4])
    done(lab.at[0], s_st.at[5])
    each(1, 4, lambda d: done(yb.at[0], s_y.at[d]))
    each(1, 4, lambda d: done(ys.at[0], s_ys.at[d]))
    each(1, 16, lambda d: done(rb.at[0], s_z1.at[d]))
    each(1, 16, lambda d: done(gb.at[0], s_z2.at[d]))
    each(0, 15, lambda i: done(R.at[0, 0], s_r.at[i]))


def on_device(teacher_hidden, teacher_head, student_hidden, student_head, labels):
    hid = teacher_hidden[0].reshape(4, 4, 512).transpose(1, 0, 2).reshape(16, 512)
    lab = jnp.broadcast_to(labels[:, None], (8, 128))
    vmem = lambda shape, dtype=F32: pltpu.VMEM(shape, dtype)
    dma = lambda n: pltpu.SemaphoreType.DMA((n,))
    space = pl.BlockSpec(memory_space=pltpu.VMEM)
    hbm = pl.BlockSpec(memory_space=pl.ANY)
    grad, ce, agree = pl.pallas_call(
        kernel,
        out_shape=(
            jax.ShapeDtypeStruct((128, 2048), F32),
            jax.ShapeDtypeStruct((16, 256), F32),
            jax.ShapeDtypeStruct((8, 256), F32),
        ),
        in_specs=[space, hbm, space, hbm, space],
        out_specs=(space,) * 3,
        scratch_shapes=[
            vmem((128, 2048), BF16), vmem((2048, 1024), BF16), vmem((8, 16, 512), BF16), vmem((256, 2048), BF16),
            vmem((256, 1024)), vmem((256, 1024), BF16), vmem((256, 1024), BF16), vmem((256, 128)), vmem((256, 128)),
            vmem((2, 4, 2, 8, 2048)), vmem((2, 4, 8, 2048)), vmem((4, 2, 8, 2048)), vmem((4, 2, 8, 2048)),
            vmem((2, 2, 8, 1024)), vmem((2, 8, 1024)), vmem((16, 1024)), vmem((2, 8, 128), I32),
            vmem((4, 4, 8, 256)), vmem((4, 2, 128)), vmem((16, 2, 256)), vmem((16, 2, 256)), vmem((16, 2, 256)),
            vmem((2, 8, 16, 1024), BF16),
            dma(PARTS), dma(6 * PARTS), dma(16 * PARTS), dma(1), dma(16), dma(12), dma(6), dma(4), dma(4), dma(16), dma(16), dma(15),
            dma(16 * PARTS), dma(8), dma(8), dma(1), dma(4), dma(1), dma(1), dma(4), dma(4), dma(16), dma(16), dma(16), dma(1), dma(1),
        ],
        compiler_params=pltpu.CompilerParams(
            collective_id=0, has_side_effects=True, vmem_limit_bytes=48 << 20
        ),
    )(hid, teacher_head, student_hidden, student_head, lab)
    z_hi = lax.axis_index("teacher") // 8
    ce = lax.dynamic_slice_in_dim(ce.reshape(16, 2, 16, 8), 8 * z_hi, 8, 2)
    agree = lax.dynamic_slice_in_dim(agree[0].reshape(2, 16, 8), 8 * z_hi, 8, 1)
    return (
        ce.transpose(2, 0, 1, 3).reshape(8, 16, 16),
        agree.transpose(1, 0, 2).reshape(8, 16),
        grad,
    )


def solution(mesh):
    return jax.shard_map(
        on_device,
        mesh=mesh,
        in_specs=(
            P("teacher", "vocab", None),
            P("teacher", "vocab"),
            P(None, "teacher"),
            P("teacher", "vocab"),
            P("teacher"),
        ),
        out_specs=(P("teacher", None, None), P("teacher", None), P("teacher", "vocab")),
        check_vma=False,
    )
```

time: 126 us -> 119 us (0.944)
  Pallas kernels: 120 us -> 113 us
    pallas_call x1, Pallas kernels: 120 us -> 113 us  [on_device(): pl.pallas_call(kernel, out_shape=(jax.ShapeDtypeStruct((128, 2048), F32),...]
where the time goes in v2:
time: 119 us
  Pallas kernels  113 us (95%)
  local copies, waits for them, and re-layouts  5.41 us (5%)
    pallas_call x1, Pallas kernels, on_device(): pl.pallas_call(kernel, out_shape=(jax.ShapeDtypeStruct((128, 2048), F32),...  113 us
    unnamed x12, local copies, waits for them, and re-layouts  4.44 us

profile of v2, /device:TPU:1, one launch (start us, length us, event | category | flops | bytes accessed | tf_op | source)
XLA Modules:
  0.0 119.2 jit_solution(2272661150329895668)
XLA Ops:
  0.6 0.0 copy-start.4
  0.6 0.0 copy-start.3
  0.7 0.0 copy-start.2
  0.7 0.6 copy-done.4
  1.3 0.1 broadcast_in_dim.2.lab_in
  1.4 0.0 copy-done.3
  1.4 0.0 copy-done.2
  1.4 0.0 copy-start
  1.4 1.0 copy-done
  2.5 0.0 copy-start.1
  2.5 1.0 copy-done.1
  3.5 113.0 %shard_map.76 = (f32[128,2048]{1,0:T(8,128)S(1)}, f32[16,256]{1,0:T(8,128)S(1)}, f32[8,256]{1,0:T(8,128)S(1)}) custom-call(bf16[16,512]{1,0:T(8,128)(2,1)S(1)} %reshape.19.hid_in, bf16[128,2048]{1,0:T(8,128)(2,1)S(1)} %copy-done, bf16[128,128]{1,0:T(8,128)(2,1)S(1)} %copy-done.2, bf16[128,2048]{1,0:T(8,128)(2,1)S(1)} %copy-done.1, ...), custom_call_target="tpu_custom_call" | custom-call | tf_op jit(solution)/shard_map/pallas_call | solution.py:372
  116.6 0.1 reshape_squeeze.7
  116.7 0.7 reshape.22
  117.4 0.1 copy.12
  117.5 0.7 copy.15
  118.2 1.0 copy.18
  (5 shorter events, 0.0 us)
Async XLA Ops:
  0.6 0.7 copy-start.4
  0.6 0.7 copy-start.3
  0.7 0.8 copy-start.2
  1.4 1.0 copy-start
  2.5 1.0 copy-start.1

commit v3 on v2

--- a/solution.py
+++ b/solution.py
@@ -12,6 +12,7 @@
 I32 = jnp.int32
 PARTS = 2
 ROWS = 128 // PARTS
+WINDOW = 2
 
 
 def iota(shape, dim):
@@ -35,6 +36,9 @@
 def own_lane(values):
     same = iota((16, 256), 0) == row_teacher(iota((16, 256), 1))
     return jnp.sum(jnp.where(same, values, 0.0), axis=0, keepdims=True)
+
+
+div, rem = lax.div, lax.rem
 
 
 def kernel(
@@ -47,13 +51,13 @@
 ):
     t = lax.axis_index("teacher")
     v = lax.axis_index("vocab")
-    zh, xc = t // 8, t % 8
-    x, c = xc // 2, xc % 2
-    zl, y = v // 4, v % 4
+    zh, xc = div(t, 8), rem(t, 8)
+    x, c = div(xc, 2), rem(xc, 2)
+    zl, y = div(v, 4), rem(v, 4)
     z = zh * 8 + zl
 
     def dev(z_, xc_, y_):
-        return {"teacher": (z_ // 8) * 8 + xc_, "vocab": (z_ % 8) * 4 + y_}
+        return {"teacher": div(z_, 8) * 8 + xc_, "vocab": rem(z_, 8) * 4 + y_}
 
     def send(src, dst, ssem, rsem, to):
         pltpu.make_async_remote_copy(
@@ -69,10 +73,10 @@
             return carry
         lax.fori_loop(lo, hi, step, 0)
 
-    z_to = lambda d: dev((z + d) % 16, xc, y)
-    x_to = lambda d: dev(z, ((x + d) % 4) * 2 + c, y)
-    y_to = lambda d: dev(z, xc, (y + d) % 4)
-    xc_to = lambda d: dev(z, (xc + d) % 8, y)
+    z_to = lambda d: dev(rem(z + d, 16), xc, y)
+    x_to = lambda d: dev(z, rem(x + d, 4) * 2 + c, y)
+    y_to = lambda d: dev(z, xc, rem(y + d, 4))
+    xc_to = lambda d: dev(z, rem(xc + d, 8), y)
     sibling = dev(z, x * 2 + 1 - c, y)
     partner = z_to(8)
 
@@ -96,7 +100,7 @@
     pltpu.make_async_copy(head.at[:, mine], block, l_w.at[0]).wait()
     pl.semaphore_wait(barrier, 25)
 
-    spread = (z % 4) * 2 + y // 2
+    spread = rem(z, 4) * 2 + div(y, 2)
     is_spread = xc == spread
     to_spread = dev(z, spread, y)
 
@@ -108,34 +112,42 @@
     def _():
         send(hid_in, hx.at[xc], s_h1.at[0], r_h1.at[xc], to_spread)
 
-    carries = y // 2 == c
+    carries = div(y, 2) == c
 
     def to_partner(part):
         p = piece(zh, x, c, part)
-        send(head.at[pl.ds(pl.multiple_of(part * ROWS, ROWS), ROWS), other], w_at(p), s_z.at[part], r_w.at[p], partner)
+        send(head.at[pl.ds(pl.multiple_of(part * ROWS, ROWS), ROWS), other], w_at(p), s_z.at[0], r_w.at[p], partner)
 
     def along_x(zg, part):
         p = piece(zg, x, c, part)
-        each(1, 4, lambda d: send(w_at(p), w_at(p), s_x.at[(zg * PARTS + part) * 3 + d - 1], r_w.at[p], x_to(d)))
-        send(w_at(p), w_at(p), s_c.at[p], r_w.at[p], sibling)
-
-    def from_x(zg):
+        each(1, 4, lambda d: send(w_at(p), w_at(p), s_x.at[0], r_w.at[p], x_to(d)))
+        send(w_at(p), w_at(p), s_c.at[0], r_w.at[p], sibling)
+
+    def from_x(zg, part):
         def go(i):
-            p = piece(zg, (x + 1 + (i % 3) * 2 % 3) % 4, c, i // 3)
+            p = piece(zg, rem(x + 1 + rem(i * 2, 3), 4), c, part)
             done(w_at(p), r_w.at[p])
-            send(w_at(p), w_at(p), s_c.at[p], r_w.at[p], sibling)
-        each(0, 3 * PARTS, go)
+            send(w_at(p), w_at(p), s_c.at[0], r_w.at[p], sibling)
+        each(0, 3, go)
 
     @pl.when(jnp.logical_not(carries))
     def _():
-        each(0, PARTS, to_partner)
+        each(0, WINDOW, to_partner)
+
+    @pl.when(carries)
+    def _():
+        to_partner(0)
     each(0, PARTS, lambda part: along_x(zh, part))
     send(S.at[:, :, 1 - c], Sc, s_st.at[0], r_sc.at[0], sibling)
 
-    k_spread = (z // 8) * 4 + ((z % 8) // 4) * 2 + y % 2
+    k_spread = div(z, 4) * 2 + rem(y, 2)
 
     def hid_at(k):
         return hid.at[pl.ds(pl.multiple_of(k * 32, 32), 32), :]
+
+    def beside(k4, k):
+        send(hid_at(k), hid_at(k), s_h2.at[0], r_h2.at[k], z_to(1))
+        send(hid_at(k), hid_at(k), s_h2.at[0], r_h2.at[k], z_to(15))
 
     @pl.when(is_spread)
     def _():
@@ -147,56 +159,74 @@
         ).astype(BF16)
         for q in range(4):
             hid[pl.ds(pl.multiple_of(k_spread * 32, 32), 32), pl.ds(q * 512, 512)] = rows[q * 32:(q + 1) * 32]
-        def go(i):
-            d = (1 - i % 2) * (i // 2 + 1) + (i % 2) * (15 - i // 2)
-            send(hid_at(k_spread), hid_at(k_spread), s_h2.at[i], r_h2.at[k_spread], z_to(d))
-        each(0, 15, go)
+        for i, d in enumerate((4, 12, 8)):
+            send(hid_at(k_spread), hid_at(k_spread), s_h2.at[0], r_h2.at[k_spread], z_to(d))
+        beside(div(z, 4), k_spread)
 
     done(Sc, r_sc.at[0])
     for h in range(2):
         for x_ in range(4):
             A[x_, h] = S[h, x_, c] + Sc[h, x_]
 
-    from_x(zh)
-    each(1, 4, lambda d: send(A.at[(x + d) % 4], Sx.at[x], s_st.at[d], r_sx.at[x], x_to(d)))
+    each(0, PARTS, lambda part: from_x(zh, part))
+    each(1, 4, lambda d: send(A.at[rem(x + d, 4)], Sx.at[x], s_st.at[1], r_sx.at[x], x_to(d)))
+
+    place = rem(z + 16 - x, 4)
 
     @pl.when(carries)
     def _():
-        def go(k4):
-            k = k4 * 2 + y % 2
-
-            @pl.when(jnp.logical_not(jnp.logical_and(is_spread, k == k_spread)))
+        def go(i):
+            k4 = rem(div(z + 17 - x, 4) + i + div(i, 2) * (1 - 2 * rem(i, 2)), 4)
+            k = k4 * 2 + rem(y, 2)
+            own = jnp.logical_and(is_spread, k == k_spread)
+
+            @pl.when(jnp.logical_not(own))
             def _():
                 done(hid_at(k), r_h2.at[k])
 
-            each(1, 4, lambda d: send(hid_at(k), hid_at(k), s_h3.at[k4 * 3 + d - 1], r_h2.at[k], y_to(d)))
+            @pl.when(jnp.logical_and(is_spread, k != k_spread))
+            def _():
+                beside(k4, k)
+
+            @pl.when(jnp.logical_and(place == 1, rem(k4, 2) == 0))
+            def _():
+                send(hid_at(k), hid_at(k), s_h2.at[0], r_h2.at[k], z_to(1))
+
+            @pl.when(jnp.logical_and(place == 3, rem(k4, 2) == 1))
+            def _():
+                send(hid_at(k), hid_at(k), s_h2.at[0], r_h2.at[k], z_to(15))
+
+            each(1, 4, lambda d: send(hid_at(k), hid_at(k), s_h3.at[0], r_h2.at[k], y_to(d)))
         each(0, 4, go)
-        each(0, PARTS, to_partner)
-
-    each(1, 4, lambda d: done(Sx.at[(x + d) % 4], r_sx.at[(x + d) % 4]))
-    total = A[x] + Sx[(x + 1) % 4] + Sx[(x + 2) % 4] + Sx[(x + 3) % 4]
+        to_partner(1)
+
+    each(1, 4, lambda d: done(Sx.at[rem(x + d, 4)], r_sx.at[rem(x + d, 4)]))
+    total = A[x] + Sx[rem(x + 1, 4)] + Sx[rem(x + 2, 4)] + Sx[rem(x + 3, 4)]
     T[0] = total[:, :, :1024]
     T[1] = total[:, :, 1024:]
 
-    def from_partner(part):
+    for part in range(PARTS):
         p = piece(1 - zh, x, c, part)
         done(w_at(p), r_w.at[p])
+        if part + WINDOW < PARTS:
+            to_partner(part + WINDOW)
         along_x(1 - zh, part)
-    each(0, PARTS, from_partner)
-    from_x(1 - zh)
+        if part > 0:
+            from_x(1 - zh, part - 1)
+    send(T.at[1 - zh], Sz, s_st.at[4], r_sz.at[0], partner)
+    send(lab.at[zh], lab.at[zh], s_st.at[5], r_lab.at[0], partner)
+    from_x(1 - zh, PARTS - 1)
 
     def last_hidden(k):
-        @pl.when(jnp.logical_not(jnp.logical_and(y // 2 == c, y % 2 == k % 2)))
+        @pl.when(jnp.logical_not(jnp.logical_and(carries, rem(y, 2) == rem(k, 2))))
         def _():
             done(hid_at(k), r_h2.at[k])
     each(0, 8, last_hidden)
 
     def from_sibling(i):
-        p = (i // PARTS) * (2 * PARTS) + (1 - c) * PARTS + i % PARTS
+        p = div(i, PARTS) * (2 * PARTS) + (1 - c) * PARTS + rem(i, PARTS)
         done(w_at(p), r_w.at[p])
     each(0, 8 * PARTS, from_sibling)
-    send(T.at[1 - zh], Sz, s_st.at[4], r_sz.at[0], partner)
-    send(lab.at[zh], lab.at[zh], s_st.at[5], r_lab.at[0], partner)
 
     def scores(n):
         cols = pl.ds(pl.multiple_of(n * 256, 256), 256)
@@ -225,7 +255,7 @@
     cross = cross + sums * local_top
     yb[y, 0:2] = cross.reshape(2, 8, 256)
     yb[y, 2:4] = jnp.concatenate([tops[:, :128], sums[:, 128:]], axis=1).reshape(2, 8, 256)
-    each(1, 4, lambda d: send(yb.at[y], yb.at[y], s_y.at[d], r_y.at[y], y_to(d)))
+    each(1, 4, lambda d: send(yb.at[y], yb.at[y], s_y.at[0], r_y.at[y], y_to(d)))
 
     done(Sz, r_sz.at[0])
     student = (T[zh] + Sz[...]).reshape(16, 1024)
@@ -236,9 +266,9 @@
     s_top = jnp.sum(jnp.where(mine_tok, s_top, 0.0), axis=0, keepdims=True)
     s_sum = jnp.sum(jnp.where(mine_tok, s_sum, 0.0), axis=0, keepdims=True)
     ys[pl.ds(y, 1)] = jnp.concatenate([s_top, s_sum], axis=0)[None]
-    each(1, 4, lambda d: send(ys.at[y], ys.at[y], s_ys.at[d], r_ys.at[y], y_to(d)))
-
-    each(1, 4, lambda d: done(yb.at[(y + d) % 4], r_y.at[(y + d) % 4]))
+    each(1, 4, lambda d: send(ys.at[y], ys.at[y], s_ys.at[0], r_ys.at[y], y_to(d)))
+
+    each(1, 4, lambda d: done(yb.at[rem(y + d, 4)], r_y.at[rem(y + d, 4)]))
     twice = lambda a: jnp.concatenate([a, a], axis=-1)
     got = yb[...]
     y_top = jnp.max(got[:, 2:4, :, :128], axis=0)
@@ -247,13 +277,41 @@
     xb[:, 0, :] = jnp.sum(got[:, 0:2] * twice(y_scale), axis=0).reshape(16, 256)
     xb[:, 1, :] = jnp.concatenate([y_top, y_sum], axis=-1).reshape(16, 256)
 
-    each(1, 16, lambda d: send(xb.at[(z + d) % 16], rb.at[z], s_z1.at[d], r_z1.at[z], z_to(d)))
+    def first_sends_left():
+        done(W.at[pl.ds(0, 128), :], s_z.at[0])
+        done(W.at[pl.ds(0, 768), :], s_x.at[0])
+        done(W.at[pl.ds(0, 1024), :], s_c.at[0])
+
+        @pl.when(jnp.logical_not(is_spread))
+        def _():
+            done(hx.at[0], s_h1.at[0])
+
+        @pl.when(is_spread)
+        def _():
+            done(W.at[pl.ds(0, 11 * 64), :], s_h2.at[0])
+
+        @pl.when(jnp.logical_and(carries, rem(place, 2) == 1))
+        def _():
+            done(W.at[pl.ds(0, 2 * 64), :], s_h2.at[0])
+
+        @pl.when(carries)
+        def _():
+            done(W.at[pl.ds(0, 12 * 64), :], s_h3.at[0])
+        done(Sc, s_st.at[0])
+        done(A.at[pl.ds(0, 3)], s_st.at[1])
+        done(Sz, s_st.at[4])
+        done(lab.at[0], s_st.at[5])
+        done(yb.at[pl.ds(0, 3)], s_y.at[0])
+        done(ys.at[pl.ds(0, 3)], s_ys.at[0])
+
+    each(1, 16, lambda d: send(xb.at[rem(z + d, 16)], rb.at[z], s_z1.at[0], r_z1.at[0], z_to(d)))
+    first_sends_left()
     rb[pl.ds(z, 1)] = xb[pl.ds(z, 1)]
-    each(1, 4, lambda d: done(ys.at[(y + d) % 4], r_ys.at[(y + d) % 4]))
+    each(1, 4, lambda d: done(ys.at[rem(y + d, 4)], r_ys.at[rem(y + d, 4)]))
     ytops, ysums = ys[:, 0, :], ys[:, 1, :]
     s_top = jnp.max(ytops, axis=0, keepdims=True)
     s_sum = jnp.sum(ysums * jnp.exp(ytops - s_top), axis=0, keepdims=True)
-    each(1, 16, lambda d: done(rb.at[(z + d) % 16], r_z1.at[(z + d) % 16]))
+    done(rb.at[pl.ds(0, 15)], r_z1.at[0])
     z_tops = rb[:, 1, :128]
     z_top = jnp.max(z_tops, axis=0, keepdims=True)
     z_scale = jnp.exp(z_tops - z_top)
@@ -261,10 +319,10 @@
     z_cross = jnp.sum(rb[:, 0, :] * twice(z_scale), axis=0, keepdims=True) / twice(z_sum)
     lane = iota((1, 256), 1)
     stud = jnp.where((lane & 1) == 0, twice(s_top), twice(s_sum))
-    z_norm = jnp.where((lane >> 7) == z // 8, twice(z_top + jnp.log(z_sum)), stud)
+    z_norm = jnp.where((lane >> 7) == zh, twice(z_top + jnp.log(z_sum)), stud)
     gb[pl.ds(z, 1)] = jnp.concatenate([z_cross, z_norm], axis=0)[None]
-    each(1, 16, lambda d: send(gb.at[z], gb.at[z], s_z2.at[d], r_z2.at[z], z_to(d)))
-    each(1, 16, lambda d: done(gb.at[(z + d) % 16], r_z2.at[(z + d) % 16]))
+    each(1, 16, lambda d: send(gb.at[z], gb.at[z], s_z2.at[0], r_z2.at[0], z_to(d)))
+    done(gb.at[pl.ds(0, 15)], r_z2.at[0])
     norms = gb[:, 1, :]
     norm = own_lane(norms)
     ce = norm - gb[:, 0, :]
@@ -301,7 +359,7 @@
     R[zh, xc] = residual.astype(BF16)
 
     def pass_r(f, xc_, i, to):
-        send(R.at[f, xc_], R.at[f, xc_], s_r.at[i], r_r.at[f * 8 + xc_], to)
+        send(R.at[f, xc_], R.at[f, xc_], s_r.at[0], r_r.at[f * 8 + xc_], to)
 
     def await_r(f, xc_):
         done(R.at[f, xc_], r_r.at[f * 8 + xc_])
@@ -312,7 +370,7 @@
 
     def relay_r(f, base):
         def go(d):
-            xc_ = ((x + d) % 4) * 2 + c
+            xc_ = (rem(x + d, 4)) * 2 + c
             await_r(f, xc_)
             pass_r(f, xc_, base + d, sibling)
         each(1, 4, go)
@@ -332,34 +390,9 @@
                 tokens, R[f, :, :, pl.ds(k * 512, 512)].reshape(128, 512),
                 (((0,), (0,)), ((), ())), preferred_element_type=F32)
 
-    each(0, PARTS, lambda i: done(w_at(0), s_z.at[i]))
-    each(0, 6 * PARTS, lambda i: done(w_at(0), s_x.at[i]))
-
-    def own_core(i):
-        p = (i // PARTS) * (2 * PARTS) + c * PARTS + i % PARTS
-        done(w_at(p), s_c.at[p])
-    each(0, 8 * PARTS, own_core)
-
-    @pl.when(jnp.logical_not(is_spread))
-    def _():
-        done(hx.at[0], s_h1.at[0])
-
-    @pl.when(is_spread)
-    def _():
-        each(0, 15, lambda d: done(hid_at(0), s_h2.at[d]))
-
-    @pl.when(y // 2 == c)
-    def _():
-        each(0, 12, lambda i: done(hid_at(0), s_h3.at[i]))
-    done(Sc, s_st.at[0])
-    each(1, 4, lambda d: done(A.at[0], s_st.at[d]))
-    done(Sz, s_st.at[4])
-    done(lab.at[0], s_st.at[5])
-    each(1, 4, lambda d: done(yb.at[0], s_y.at[d]))
-    each(1, 4, lambda d: done(ys.at[0], s_ys.at[d]))
-    each(1, 16, lambda d: done(rb.at[0], s_z1.at[d]))
-    each(1, 16, lambda d: done(gb.at[0], s_z2.at[d]))
-    each(0, 15, lambda i: done(R.at[0, 0], s_r.at[i]))
+    done(xb.at[pl.ds(0, 15)], s_z1.at[0])
+    done(gb.at[pl.ds(0, 15)], s_z2.at[0])
+    done(W.at[pl.ds(0, 240), :], s_r.at[0])
 
 
 def on_device(teacher_hidden, teacher_head, student_hidden, student_head, labels):
@@ -385,8 +418,9 @@
             vmem((2, 2, 8, 1024)), vmem((2, 8, 1024)), vmem((16, 1024)), vmem((2, 8, 128), I32),
             vmem((4, 4, 8, 256)), vmem((4, 2, 128)), vmem((16, 2, 256)), vmem((16, 2, 256)), vmem((16, 2, 256)),
             vmem((2, 8, 16, 1024), BF16),
-            dma(PARTS), dma(6 * PARTS), dma(16 * PARTS), dma(1), dma(16), dma(12), dma(6), dma(4), dma(4), dma(16), dma(16), dma(15),
-            dma(16 * PARTS), dma(8), dma(8), dma(1), dma(4), dma(1), dma(1), dma(4), dma(4), dma(16), dma(16), dma(16), dma(1), dma(1),
+            dma(1), dma(1), dma(1), dma(1), dma(1), dma(1), dma(6), dma(1), dma(1), dma(1), dma(1), dma(1),
+            dma(16 * PARTS), dma(8), dma(8), dma(1), dma(4), dma(1), dma(1), dma(4), dma(4), dma(1), dma(1), dma(16),
+            dma(1), dma(1),
         ],
         compiler_params=pltpu.CompilerParams(
             collective_id=0, has_side_effects=True, vmem_limit_bytes=48 << 20

time: 119 us -> 114 us (0.958)
  Pallas kernels: 113 us -> 107 us
    pallas_call x1, Pallas kernels: 113 us -> 107 us  [on_device(): pl.pallas_call(kernel, out_shape=(jax.ShapeDtypeStruct((128, 2048), F32),...]
where the time goes in v3:
time: 114 us; the launch traced here: 113 us
  Pallas kernels  107 us (94%)
  local copies, waits for them, and re-layouts  5.41 us (5%)
    pallas_call x1, Pallas kernels, on_device(): pl.pallas_call(kernel, out_shape=(jax.ShapeDtypeStruct((128, 2048), F32),...  107 us
    unnamed x12, local copies, waits for them, and re-layouts  4.44 us

profile of v3, /device:TPU:1, one launch (start us, length us, event | category | flops | bytes accessed | tf_op | source)
XLA Modules:
  0.0 113.4 jit_solution(14623648096287341562)
XLA Ops:
  0.6 0.0 copy-start.4
  0.6 0.0 copy-start.3
  0.7 0.0 copy-start.2
  0.7 0.6 copy-done.4
  1.3 0.1 broadcast_in_dim.2.lab_in
  1.4 0.0 copy-done.3
  1.4 0.0 copy-done.2
  1.4 0.0 copy-start
  1.4 1.0 copy-done
  2.5 0.0 copy-start.1
  2.5 1.0 copy-done.1
  3.5 107.3 %shard_map.76 = (f32[128,2048]{1,0:T(8,128)S(1)}, f32[16,256]{1,0:T(8,128)S(1)}, f32[8,256]{1,0:T(8,128)S(1)}) custom-call(bf16[16,512]{1,0:T(8,128)(2,1)S(1)} %reshape.19.hid_in, bf16[128,2048]{1,0:T(8,128)(2,1)S(1)} %copy-done, bf16[128,128]{1,0:T(8,128)(2,1)S(1)} %copy-done.2, bf16[128,2048]{1,0:T(8,128)(2,1)S(1)} %copy-done.1, ...), custom_call_target="tpu_custom_call" | custom-call | tf_op jit(solution)/shard_map/pallas_call | solution.py:405
  110.9 0.1 reshape_squeeze.7
  111.0 0.7 reshape.22
  111.6 0.1 copy.12
  111.8 0.7 copy.15
  112.5 1.0 copy.18
  (5 shorter events, 0.0 us)
Async XLA Ops:
  0.6 0.7 copy-start.4
  0.6 0.7 copy-start.3
  0.7 0.8 copy-start.2
  1.4 1.0 copy-start
  2.5 1.0 copy-start.1

commit v4 on v3

--- a/solution.py
+++ b/solution.py
@@ -73,6 +73,9 @@
             return carry
         lax.fori_loop(lo, hi, step, 0)
 
+    def far_first(body):
+        each(0, 15, lambda i: body(8 + div(i, 2) * (1 - 2 * rem(i, 2)) - rem(i, 2)))
+
     z_to = lambda d: dev(rem(z + d, 16), xc, y)
     x_to = lambda d: dev(z, rem(x + d, 4) * 2 + c, y)
     y_to = lambda d: dev(z, xc, rem(y + d, 4))
@@ -215,23 +218,32 @@
             from_x(1 - zh, part - 1)
     send(T.at[1 - zh], Sz, s_st.at[4], r_sz.at[0], partner)
     send(lab.at[zh], lab.at[zh], s_st.at[5], r_lab.at[0], partner)
+    def from_sibling(zg):
+        def go(i):
+            p = (zg * 8 + div(i, PARTS) * 2 + 1 - c) * PARTS + rem(i, PARTS)
+            done(w_at(p), r_w.at[p])
+        each(0, 4 * PARTS, go)
+
+    def scores(zg, add):
+        depth = pl.ds(pl.multiple_of(zg * 1024, 1024), 1024)
+
+        def go(n):
+            cols = pl.ds(pl.multiple_of(n * 256, 256), 256)
+            part = jnp.dot(hid[:, depth], W[depth, cols], preferred_element_type=F32)
+            L[:, cols] = L[:, cols] + part if add else part
+        each(0, 4, go)
+
     from_x(1 - zh, PARTS - 1)
-
     def last_hidden(k):
         @pl.when(jnp.logical_not(jnp.logical_and(carries, rem(y, 2) == rem(k, 2))))
         def _():
             done(hid_at(k), r_h2.at[k])
     each(0, 8, last_hidden)
-
-    def from_sibling(i):
-        p = div(i, PARTS) * (2 * PARTS) + (1 - c) * PARTS + rem(i, PARTS)
-        done(w_at(p), r_w.at[p])
-    each(0, 8 * PARTS, from_sibling)
-
-    def scores(n):
-        cols = pl.ds(pl.multiple_of(n * 256, 256), 256)
-        L[:, cols] = jnp.dot(hid[...], W[:, cols], preferred_element_type=F32)
-    each(0, 4, scores)
+    from_sibling(zh)
+    scores(zh, False)
+
+    from_sibling(1 - zh)
+    scores(1 - zh, True)
 
     def local_stats(n):
         rows = pl.ds(pl.multiple_of(n * 32, 32), 32)
@@ -304,7 +316,7 @@
         done(yb.at[pl.ds(0, 3)], s_y.at[0])
         done(ys.at[pl.ds(0, 3)], s_ys.at[0])
 
-    each(1, 16, lambda d: send(xb.at[rem(z + d, 16)], rb.at[z], s_z1.at[0], r_z1.at[0], z_to(d)))
+    far_first(lambda d: send(xb.at[rem(z + d, 16)], rb.at[z], s_z1.at[0], r_z1.at[0], z_to(d)))
     first_sends_left()
     rb[pl.ds(z, 1)] = xb[pl.ds(z, 1)]
     each(1, 4, lambda d: done(ys.at[rem(y + d, 4)], r_ys.at[rem(y + d, 4)]))
@@ -321,7 +333,7 @@
     stud = jnp.where((lane & 1) == 0, twice(s_top), twice(s_sum))
     z_norm = jnp.where((lane >> 7) == zh, twice(z_top + jnp.log(z_sum)), stud)
     gb[pl.ds(z, 1)] = jnp.concatenate([z_cross, z_norm], axis=0)[None]
-    each(1, 16, lambda d: send(gb.at[z], gb.at[z], s_z2.at[0], r_z2.at[0], z_to(d)))
+    far_first(lambda d: send(gb.at[z], gb.at[z], s_z2.at[0], r_z2.at[0], z_to(d)))
     done(gb.at[pl.ds(0, 15)], r_z2.at[0])
     norms = gb[:, 1, :]
     norm = own_lane(norms)
@@ -378,17 +390,20 @@
     relay_r(zh, 4)
     tokens = sh[...].astype(F32).reshape(2, 8, 8, 128)
     tokens = jnp.swapaxes(tokens, 0, 1).reshape(128, 128).astype(BF16)
+
+    def grad(f):
+        each(0, 4, lambda i: await_r(f, i * 2 + 1 - c))
+        for k in range(2):
+            cols = pl.ds(pl.multiple_of(f * 1024 + k * 512, 512), 512)
+            grad_out[:, cols] = lax.dot_general(
+                tokens, R[f, :, :, pl.ds(k * 512, 512)].reshape(128, 512),
+                (((0,), (0,)), ((), ())), preferred_element_type=F32)
+    grad(zh)
     await_r(1 - zh, xc)
     each(1, 4, lambda d: pass_r(1 - zh, xc, 7 + d, x_to(d)))
     pass_r(1 - zh, xc, 11, sibling)
     relay_r(1 - zh, 11)
-    for f in range(2):
-        each(0, 4, lambda i: await_r(f, i * 2 + 1 - c))
-    for f in range(2):
-        for k in range(2):
-            grad_out[:, pl.ds(f * 1024 + k * 512, 512)] = lax.dot_general(
-                tokens, R[f, :, :, pl.ds(k * 512, 512)].reshape(128, 512),
-                (((0,), (0,)), ((), ())), preferred_element_type=F32)
+    grad(1 - zh)
 
     done(xb.at[pl.ds(0, 15)], s_z1.at[0])
     done(gb.at[pl.ds(0, 15)], s_z2.at[0])

time: 114 us -> 112 us (0.982)
    pallas_call x1, Pallas kernels: 107 us -> 106 us  [on_device(): pl.pallas_call(kernel, out_shape=(jax.ShapeDtypeStruct((128, 2048), F32),...]
where the time goes in v4:
time: 112 us
  Pallas kernels  106 us (95%)
  local copies, waits for them, and re-layouts  5.41 us (5%)
    pallas_call x1, Pallas kernels, on_device(): pl.pallas_call(kernel, out_shape=(jax.ShapeDtypeStruct((128, 2048), F32),...  106 us
    unnamed x12, local copies, waits for them, and re-layouts  4.44 us

profile of v4, /device:TPU:1, one launch (start us, length us, event | category | flops | bytes accessed | tf_op | source)
XLA Modules:
  0.0 111.7 jit_solution(1456477217241864168)
XLA Ops:
  0.6 0.0 copy-start.4
  0.6 0.0 copy-start.3
  0.7 0.0 copy-start.2
  0.7 0.6 copy-done.4
  1.3 0.1 broadcast_in_dim.2.lab_in
  1.4 0.0 copy-done.3
  1.4 0.0 copy-done.2
  1.4 0.0 copy-start
  1.4 1.0 copy-done
  2.5 0.0 copy-start.1
  2.5 1.0 copy-done.1
  3.5 105.6 %shard_map.76 = (f32[128,2048]{1,0:T(8,128)S(1)}, f32[16,256]{1,0:T(8,128)S(1)}, f32[8,256]{1,0:T(8,128)S(1)}) custom-call(bf16[16,512]{1,0:T(8,128)(2,1)S(1)} %reshape.19.hid_in, bf16[128,2048]{1,0:T(8,128)(2,1)S(1)} %copy-done, bf16[128,128]{1,0:T(8,128)(2,1)S(1)} %copy-done.2, bf16[128,2048]{1,0:T(8,128)(2,1)S(1)} %copy-done.1, ...), custom_call_target="tpu_custom_call" | custom-call | tf_op jit(solution)/shard_map/pallas_call | solution.py:420
  109.1 0.1 reshape_squeeze.7
  109.2 0.7 reshape.22
  109.9 0.1 copy.12
  110.0 0.7 copy.15
  110.7 1.0 copy.18
  (5 shorter events, 0.0 us)
Async XLA Ops:
  0.6 0.7 copy-start.4
  0.6 0.7 copy-start.3
  0.7 0.8 copy-start.2
  1.4 1.0 copy-start
  2.5 1.0 copy-start.1

commit v5 on v4

--- a/solution.py
+++ b/solution.py
@@ -269,6 +269,44 @@
     yb[y, 2:4] = jnp.concatenate([tops[:, :128], sums[:, 128:]], axis=1).reshape(2, 8, 256)
     each(1, 4, lambda d: send(yb.at[y], yb.at[y], s_y.at[0], r_y.at[y], y_to(d)))
 
+    each(1, 4, lambda d: done(yb.at[rem(y + d, 4)], r_y.at[rem(y + d, 4)]))
+    twice = lambda a: jnp.concatenate([a, a], axis=-1)
+    got = yb[...]
+    y_top = jnp.max(got[:, 2:4, :, :128], axis=0)
+    y_scale = jnp.exp(got[:, 2:4, :, :128] - y_top[None])
+    y_sum = jnp.sum(got[:, 2:4, :, 128:] * y_scale, axis=0)
+    xb[:, 0, :] = jnp.sum(got[:, 0:2] * twice(y_scale), axis=0).reshape(16, 256)
+    xb[:, 1, :] = jnp.concatenate([y_top, y_sum], axis=-1).reshape(16, 256)
+
+    def first_sends_left():
+        done(W.at[pl.ds(0, 128), :], s_z.at[0])
+        done(W.at[pl.ds(0, 768), :], s_x.at[0])
+        done(W.at[pl.ds(0, 1024), :], s_c.at[0])
+
+        @pl.when(jnp.logical_not(is_spread))
+        def _():
+            done(hx.at[0], s_h1.at[0])
+
+        @pl.when(is_spread)
+        def _():
+            done(W.at[pl.ds(0, 11 * 64), :], s_h2.at[0])
+
+        @pl.when(jnp.logical_and(carries, rem(place, 2) == 1))
+        def _():
+            done(W.at[pl.ds(0, 2 * 64), :], s_h2.at[0])
+
+        @pl.when(carries)
+        def _():
+            done(W.at[pl.ds(0, 12 * 64), :], s_h3.at[0])
+        done(Sc, s_st.at[0])
+        done(A.at[pl.ds(0, 3)], s_st.at[1])
+        done(Sz, s_st.at[4])
+        done(lab.at[0], s_st.at[5])
+        done(yb.at[pl.ds(0, 3)], s_y.at[0])
+        done(ys.at[pl.ds(0, 3)], s_ys.at[0])
+
+    far_first(lambda d: send(xb.at[rem(z + d, 16)], rb.at[z], s_z1.at[0], r_z1.at[0], z_to(d)))
+
     done(Sz, r_sz.at[0])
     student = (T[zh] + Sz[...]).reshape(16, 1024)
     SL[...] = student
@@ -280,44 +318,6 @@
     ys[pl.ds(y, 1)] = jnp.concatenate([s_top, s_sum], axis=0)[None]
     each(1, 4, lambda d: send(ys.at[y], ys.at[y], s_ys.at[0], r_ys.at[y], y_to(d)))
 
-    each(1, 4, lambda d: done(yb.at[rem(y + d, 4)], r_y.at[rem(y + d, 4)]))
-    twice = lambda a: jnp.concatenate([a, a], axis=-1)
-    got = yb[...]
-    y_top = jnp.max(got[:, 2:4, :, :128], axis=0)
-    y_scale = jnp.exp(got[:, 2:4, :, :128] - y_top[None])
-    y_sum = jnp.sum(got[:, 2:4, :, 128:] * y_scale, axis=0)
-    xb[:, 0, :] = jnp.sum(got[:, 0:2] * twice(y_scale), axis=0).reshape(16, 256)
-    xb[:, 1, :] = jnp.concatenate([y_top, y_sum], axis=-1).reshape(16, 256)
-
-    def first_sends_left():
-        done(W.at[pl.ds(0, 128), :], s_z.at[0])
-        done(W.at[pl.ds(0, 768), :], s_x.at[0])
-        done(W.at[pl.ds(0, 1024), :], s_c.at[0])
-
-        @pl.when(jnp.logical_not(is_spread))
-        def _():
-            done(hx.at[0], s_h1.at[0])
-
-        @pl.when(is_spread)
-        def _():
-            done(W.at[pl.ds(0, 11 * 64), :], s_h2.at[0])
-
-        @pl.when(jnp.logical_and(carries, rem(place, 2) == 1))
-        def _():
-            done(W.at[pl.ds(0, 2 * 64), :], s_h2.at[0])
-
-        @pl.when(carries)
-        def _():
-            done(W.at[pl.ds(0, 12 * 64), :], s_h3.at[0])
-        done(Sc, s_st.at[0])
-        done(A.at[pl.ds(0, 3)], s_st.at[1])
-        done(Sz, s_st.at[4])
-        done(lab.at[0], s_st.at[5])
-        done(yb.at[pl.ds(0, 3)], s_y.at[0])
-        done(ys.at[pl.ds(0, 3)], s_ys.at[0])
-
-    far_first(lambda d: send(xb.at[rem(z + d, 16)], rb.at[z], s_z1.at[0], r_z1.at[0], z_to(d)))
-    first_sends_left()
     rb[pl.ds(z, 1)] = xb[pl.ds(z, 1)]
     each(1, 4, lambda d: done(ys.at[rem(y + d, 4)], r_ys.at[rem(y + d, 4)]))
     ytops, ysums = ys[:, 0, :], ys[:, 1, :]
@@ -405,6 +405,7 @@
     relay_r(1 - zh, 11)
     grad(1 - zh)
 
+    first_sends_left()
     done(xb.at[pl.ds(0, 15)], s_z1.at[0])
     done(gb.at[pl.ds(0, 15)], s_z2.at[0])
     done(W.at[pl.ds(0, 240), :], s_r.at[0])

time: 112 us -> 112 us (level)
  no operation moved by 1% of the time
where the time goes in v5:
time: 112 us
  Pallas kernels  106 us (95%)
  local copies, waits for them, and re-layouts  5.41 us (5%)
    pallas_call x1, Pallas kernels, on_device(): pl.pallas_call(kernel, out_shape=(jax.ShapeDtypeStruct((128, 2048), F32),...  106 us
    unnamed x12, local copies, waits for them, and re-layouts  4.44 us

profile of v5, /device:TPU:1, one launch (start us, length us, event | category | flops | bytes accessed | tf_op | source)
XLA Modules:
  0.0 111.7 jit_solution(2065368058328164996)
XLA Ops:
  0.6 0.0 copy-start.4
  0.6 0.0 copy-start.3
  0.7 0.0 copy-start.2
  0.7 0.6 copy-done.4
  1.3 0.1 broadcast_in_dim.2.lab_in
  1.4 0.0 copy-done.3
  1.4 0.0 copy-done.2
  1.4 0.0 copy-start
  1.4 1.0 copy-done
  2.5 0.0 copy-start.1
  2.5 1.0 copy-done.1
  3.5 105.6 %shard_map.76 = (f32[128,2048]{1,0:T(8,128)S(1)}, f32[16,256]{1,0:T(8,128)S(1)}, f32[8,256]{1,0:T(8,128)S(1)}) custom-call(bf16[16,512]{1,0:T(8,128)(2,1)S(1)} %reshape.19.hid_in, bf16[128,2048]{1,0:T(8,128)(2,1)S(1)} %copy-done, bf16[128,128]{1,0:T(8,128)(2,1)S(1)} %copy-done.2, bf16[128,2048]{1,0:T(8,128)(2,1)S(1)} %copy-done.1, ...), custom_call_target="tpu_custom_call" | custom-call | tf_op jit(solution)/shard_map/pallas_call | solution.py:421
  109.1 0.1 reshape_squeeze.7
  109.2 0.7 reshape.22
  109.9 0.1 copy.12
  110.0 0.7 copy.15
  110.7 1.0 copy.18
  (5 shorter events, 0.0 us)
Async XLA Ops:
  0.6 0.7 copy-start.4
  0.6 0.7 copy-start.3
  0.7 0.8 copy-start.2
  1.4 1.0 copy-start
  2.5 1.0 copy-start.1
